TPU v7x, 32 devices: a whole 2x2x4 slice. The times are simulated.
32 devices in a mesh: fsdp: 2 (over x), seq: 16 (over z, y, core).
Axes of the slice: x: 2, y: 2, z: 4, core: 2. Of those that a mesh axis runs over, the one named last changes fastest.
Arguments:
- hidden_in: bfloat16 [8192, 640], P(('fsdp', 'seq')), may hold values from -6 to 6
- cotangent: bfloat16 [8192, 640], P(('fsdp', 'seq')), may hold values from -6 to 6
- dataset_ids: int32 [8192], P(('fsdp', 'seq')), may hold values from 0 to 15
- mixing: float32 [16], replicated, may hold values from 0.25 to 4
- pad_lengths: int32 [2], P('fsdp'), may hold values from 0 to 2047
- attention_gain: bfloat16 [640], P(('fsdp', 'seq')), may hold values from 0.5 to 1.5
- merged_projection: bfloat16 [640, 1536], P(('fsdp', 'seq')), may hold values from -0.25 to 0.25
- merged_adapter_in: bfloat16 [640, 768], P(('fsdp', 'seq')), may hold values from -0.25 to 0.25
- query_adapter_out: bfloat16 [256, 1024], P(('fsdp', 'seq')), may hold values from -0.375 to 0.375
- keyval_adapter_out: bfloat16 [512, 256], P(('fsdp', 'seq')), may hold values from -0.375 to 0.375
- output_projection: bfloat16 [1024, 640], P(('fsdp', 'seq')), may hold values from -4 to 4
- output_adapter_in: bfloat16 [1024, 256], P(('fsdp', 'seq')), may hold values from -4 to 4
- output_adapter_out: bfloat16 [256, 640], P(('fsdp', 'seq')), may hold values from -0.375 to 0.375
- feedforward_gain: bfloat16 [640], P(('fsdp', 'seq')), may hold values from 0.5 to 1.5
- gate_up_weight: bfloat16 [640, 4096], P(('fsdp', 'seq')), may hold values from -0.25 to 0.25
- gate_up_adapter_in: bfloat16 [640, 512], P(('fsdp', 'seq')), may hold values from -0.25 to 0.25
- gate_up_adapter_out: bfloat16 [512, 2048], P(('fsdp', 'seq')), may hold values from -0.375 to 0.375
- down_weight: bfloat16 [2048, 640], P(('fsdp', 'seq')), may hold values from -0.125 to 0.125
- down_adapter_in: bfloat16 [2048, 256], P(('fsdp', 'seq')), may hold values from -0.125 to 0.125
- down_adapter_out: bfloat16 [256, 640], P(('fsdp', 'seq')), may hold values from -0.375 to 0.375
Outputs:
- output: bfloat16 [8192, 640], P(('fsdp', 'seq'))
- hidden_grad: bfloat16 [8192, 640], P(('fsdp', 'seq'))
- attention_gain_grad: float32 [640], P(('fsdp', 'seq'))
- merged_projection_grad: float32 [640, 1536], P(('fsdp', 'seq'))
- merged_adapter_in_grad: float32 [640, 768], P(('fsdp', 'seq'))
- query_adapter_out_grad: float32 [256, 1024], P(('fsdp', 'seq'))
- keyval_adapter_out_grad: float32 [512, 256], P(('fsdp', 'seq'))
- output_projection_grad: float32 [1024, 640], P(('fsdp', 'seq'))
- output_adapter_in_grad: float32 [1024, 256], P(('fsdp', 'seq'))
- output_adapter_out_grad: float32 [256, 640], P(('fsdp', 'seq'))
- feedforward_gain_grad: float32 [640], P(('fsdp', 'seq'))
- gate_up_weight_grad: float32 [640, 4096], P(('fsdp', 'seq'))
- gate_up_adapter_in_grad: float32 [640, 512], P(('fsdp', 'seq'))
- gate_up_adapter_out_grad: float32 [512, 2048], P(('fsdp', 'seq'))
- down_weight_grad: float32 [2048, 640], P(('fsdp', 'seq'))
- down_adapter_in_grad: float32 [2048, 256], P(('fsdp', 'seq'))
- down_adapter_out_grad: float32 [256, 640], P(('fsdp', 'seq'))
All inputs are finite; a program needn't handle non-finite values.
Results may differ from a plain program's by a relative error of at most 0.019.
The roundings to bfloat16 on the way count: a program that leaves them out, or rounds other values in their place, can miss the bound.
Values may be sent and summed in bfloat16 or wider, within the bound.
A program may use at most 192 MiB of HBM per device.

v0:
```python
from functools import partial

import jax
import jax.numpy as jnp
from jax import lax
from jax.sharding import PartitionSpec as P

HEADS = 4
HEAD_DIM = 256
FF = 2048
RANK = 256
DATASETS = 16


EPSILON = 1e-06


def rms_scale(values, gain_vector):
    inverse = lax.rsqrt(jnp.mean(values * values, axis=-1, keepdims=True) + EPSILON)
    return values * inverse * gain_vector


def rotary_tables(positions):
    half_width = HEAD_DIM // 2
    inverse = 10000.0 ** (-2.0 * jnp.arange(half_width, dtype=jnp.float32) / HEAD_DIM)
    angles = positions.astype(jnp.float32)[:, None] * inverse[None, :]
    return (jnp.cos(angles), jnp.sin(angles))


def rotate(values, cosine_table, sine_table):
    half_width = values.shape[-1] // 2
    first = values[..., :half_width]
    second = values[..., half_width:]
    return jnp.concatenate(
        [first * cosine_table - second * sine_table, second * cosine_table + first * sine_table],
        axis=-1,
    )


def rotate_back(values, cosine_table, sine_table):
    half_width = values.shape[-1] // 2
    first = values[..., :half_width]
    second = values[..., half_width:]
    return jnp.concatenate(
        [first * cosine_table + second * sine_table, second * cosine_table - first * sine_table],
        axis=-1,
    )


def matmul(left_side, right_side):
    return jnp.dot(left_side, right_side, preferred_element_type=jnp.float32)


def times_transposed(left_side, right_side):
    return lax.dot_general(
        left_side, right_side, (((1,), (1,)), ((), ())), preferred_element_type=jnp.float32
    )


def transposed_times(left_side, right_side):
    return lax.dot_general(
        left_side, right_side, (((0,), (0,)), ((), ())), preferred_element_type=jnp.float32
    )


def weight_gradient(activations, gradients, shard_rows):
    return lax.psum_scatter(
        transposed_times(
            lax.slice_in_dim(activations, 0, shard_rows * lax.axis_size(("fsdp", "seq")), axis=1),
            gradients,
        ),
        ("fsdp", "seq"),
        scatter_dimension=0,
        tiled=True,
    )


def per_device(
    hidden_in,
    cotangent,
    dataset_ids,
    mixing,
    pad_lengths,
    attention_gain,
    merged_projection,
    merged_adapter_in,
    query_adapter_out,
    keyval_adapter_out,
    output_projection,
    output_adapter_in,
    output_adapter_out,
    feedforward_gain,
    gate_up_weight,
    gate_up_adapter_in,
    gate_up_adapter_out,
    down_weight,
    down_adapter_in,
    down_adapter_out,
):
    tokens = hidden_in.shape[0]
    query_width = HEADS * HEAD_DIM
    scale = HEAD_DIM ** (-0.5)
    gain_one, merged_full, adapt_merged, lift_query, lift_keyval, out_full, adapt_out, lift_out = (
        lax.all_gather(attention_gain, ("fsdp", "seq"), axis=0, tiled=True),
        lax.all_gather(merged_projection, ("fsdp", "seq"), axis=0, tiled=True),
        lax.all_gather(merged_adapter_in, ("fsdp", "seq"), axis=0, tiled=True),
        lax.all_gather(query_adapter_out, ("fsdp", "seq"), axis=0, tiled=True),
        lax.all_gather(keyval_adapter_out, ("fsdp", "seq"), axis=0, tiled=True),
        lax.all_gather(output_projection, ("fsdp", "seq"), axis=0, tiled=True),
        lax.all_gather(output_adapter_in, ("fsdp", "seq"), axis=0, tiled=True),
        lax.all_gather(output_adapter_out, ("fsdp", "seq"), axis=0, tiled=True),
    )
    hidden = hidden_in.astype(jnp.float32)
    normed_one, norm_one_back = jax.vjp(rms_scale, hidden, gain_one.astype(jnp.float32))
    first_in = normed_one.astype(jnp.bfloat16)
    projected = matmul(first_in, merged_full)
    lifted = matmul(first_in, adapt_merged).astype(jnp.bfloat16)
    query_rows = projected[:, :query_width] + matmul(lifted[:, :RANK], lift_query)
    key_rows = projected[:, query_width : query_width + HEAD_DIM] + matmul(
        lifted[:, RANK : 2 * RANK], lift_keyval[:RANK]
    )
    value_rows = projected[:, query_width + HEAD_DIM :] + matmul(
        lifted[:, 2 * RANK :], lift_keyval[RANK:]
    )
    start_pos = lax.axis_index("seq") * tokens
    positions = start_pos + jnp.arange(tokens, dtype=jnp.int32)
    cosine_table, sine_table = rotary_tables(positions)
    query_rot = (
        rotate(
            query_rows.reshape(tokens, HEADS, HEAD_DIM),
            cosine_table[:, None, :],
            sine_table[:, None, :],
        )
        .astype(jnp.bfloat16)
        .reshape(tokens * HEADS, HEAD_DIM)
    )
    keys_rot = rotate(key_rows, cosine_table, sine_table).astype(jnp.bfloat16)
    values_low = value_rows.astype(jnp.bfloat16)
    keys_all, values_all = (
        lax.all_gather(keys_rot, "seq", axis=0, tiled=True),
        lax.all_gather(values_low, "seq", axis=0, tiled=True),
    )
    length = keys_all.shape[0]
    valid_count = length - pad_lengths[0]
    key_span = min(512, length)
    block_count = length // key_span
    key_blocks = keys_all.reshape(block_count, key_span, HEAD_DIM)
    value_blocks = values_all.reshape(block_count, key_span, HEAD_DIM)
    block_starts = jnp.arange(block_count, dtype=jnp.int32) * key_span
    row_pos = start_pos + jnp.arange(tokens * HEADS, dtype=jnp.int32) // HEADS
    last_pos = start_pos + tokens - 1

    def scores_of(key_block, block_start):
        raw_scores = times_transposed(query_rot, key_block) * scale
        key_pos = block_start + jnp.arange(key_span, dtype=jnp.int32)
        allowed = (key_pos[None, :] <= row_pos[:, None]) & (key_pos[None, :] < valid_count)
        return (raw_scores, allowed)

    def blockwise(step, initial, empty_out):

        def guarded(carry_state, block_item):

            def passing(state_in, item_in):
                return (state_in, empty_out)

            live_block = (block_item[0] <= last_pos) & (block_item[0] < valid_count)
            return lax.cond(live_block, step, passing, carry_state, block_item)

        return lax.scan(guarded, initial, (block_starts, key_blocks, value_blocks))

    def stats_step(carry_state, block_item):
        row_peak, row_total = carry_state
        raw_scores, allowed = scores_of(block_item[1], block_item[0])
        masked = jnp.where(allowed, raw_scores, -jnp.inf)
        new_peak = jnp.maximum(row_peak, jnp.max(masked, axis=1))
        row_total = row_total * jnp.exp(row_peak - new_peak) + jnp.sum(
            jnp.exp(masked - new_peak[:, None]), axis=1
        )
        return ((new_peak, row_total), None)

    row_total_count = tokens * HEADS
    (row_peak, row_total), unused = blockwise(
        stats_step,
        (
            jnp.full((row_total_count,), -jnp.inf, jnp.float32),
            jnp.zeros((row_total_count,), jnp.float32),
        ),
        None,
    )
    log_norm = row_peak + jnp.log(row_total)

    def output_step(running, block_item):
        raw_scores, allowed = scores_of(block_item[1], block_item[0])
        soft_weights = jnp.where(allowed, jnp.exp(raw_scores - log_norm[:, None]), 0.0).astype(
            jnp.bfloat16
        )
        return (running + matmul(soft_weights, block_item[2]), None)

    attention_out, unused = blockwise(
        output_step, jnp.zeros((row_total_count, HEAD_DIM), jnp.float32), None
    )
    attention_low = attention_out.astype(jnp.bfloat16).reshape(tokens, query_width)
    out_base = matmul(attention_low, out_full)
    lifted_out = matmul(attention_low, adapt_out).astype(jnp.bfloat16)
    middle = hidden + (out_base + matmul(lifted_out, lift_out))
    gain_two, gate_up_full, adapt_gate_up, lift_gate_up, down_full, adapt_down, lift_down = (
        lax.all_gather(feedforward_gain, ("fsdp", "seq"), axis=0, tiled=True),
        lax.all_gather(gate_up_weight, ("fsdp", "seq"), axis=0, tiled=True),
        lax.all_gather(gate_up_adapter_in, ("fsdp", "seq"), axis=0, tiled=True),
        lax.all_gather(gate_up_adapter_out, ("fsdp", "seq"), axis=0, tiled=True),
        lax.all_gather(down_weight, ("fsdp", "seq"), axis=0, tiled=True),
        lax.all_gather(down_adapter_in, ("fsdp", "seq"), axis=0, tiled=True),
        lax.all_gather(down_adapter_out, ("fsdp", "seq"), axis=0, tiled=True),
    )
    normed_two, norm_two_back = jax.vjp(rms_scale, middle, gain_two.astype(jnp.float32))
    second_in = normed_two.astype(jnp.bfloat16)
    pre_gate = matmul(second_in, gate_up_full)
    lifted_gate_up = matmul(second_in, adapt_gate_up).astype(jnp.bfloat16)
    gate_part = pre_gate[:, :FF] + matmul(lifted_gate_up[:, :RANK], lift_gate_up[:RANK])
    upper_part = pre_gate[:, FF:] + matmul(lifted_gate_up[:, RANK:], lift_gate_up[RANK:])
    activated, gelu_back = jax.vjp(partial(jax.nn.gelu, approximate=True), gate_part)
    inner = (activated * upper_part).astype(jnp.bfloat16)
    down_base = matmul(inner, down_full)
    lifted_down = matmul(inner, adapt_down).astype(jnp.bfloat16)
    output = middle + (down_base + matmul(lifted_down, lift_down))
    matches = dataset_ids[:, None] == jnp.arange(DATASETS, dtype=jnp.int32)[None, :]
    picked = jnp.sum(jnp.where(matches, mixing[None, :], 0.0), axis=1)
    row_weight = jnp.where(positions < valid_count, picked, 0.0)
    scaled = cotangent.astype(jnp.float32) * row_weight[:, None]
    (
        gate_up_again,
        adapt_gate_up_again,
        lift_gate_up_again,
        down_again,
        adapt_down_again,
        lift_down_again,
    ) = (
        lax.all_gather(gate_up_weight, ("fsdp", "seq"), axis=0, tiled=True),
        lax.all_gather(gate_up_adapter_in, ("fsdp", "seq"), axis=0, tiled=True),
        lax.all_gather(gate_up_adapter_out, ("fsdp", "seq"), axis=0, tiled=True),
        lax.all_gather(down_weight, ("fsdp", "seq"), axis=0, tiled=True),
        lax.all_gather(down_adapter_in, ("fsdp", "seq"), axis=0, tiled=True),
        lax.all_gather(down_adapter_out, ("fsdp", "seq"), axis=0, tiled=True),
    )
    grad_branch = scaled.astype(jnp.bfloat16)
    grad_lifted_down = times_transposed(grad_branch, lift_down_again).astype(jnp.bfloat16)
    grad_inner = times_transposed(grad_branch, down_again) + times_transposed(
        grad_lifted_down, adapt_down_again
    )
    grad_gate = gelu_back(grad_inner * upper_part)[0]
    grad_upper = grad_inner * activated
    grad_gate_up = jnp.concatenate([grad_gate, grad_upper], axis=1).astype(jnp.bfloat16)
    grad_lifted_gate_up = jnp.concatenate(
        [
            times_transposed(grad_gate_up[:, :FF], lift_gate_up_again[:RANK]),
            times_transposed(grad_gate_up[:, FF:], lift_gate_up_again[RANK:]),
        ],
        axis=1,
    ).astype(jnp.bfloat16)
    grad_normed_two = times_transposed(grad_gate_up, gate_up_again) + times_transposed(
        grad_lifted_gate_up, adapt_gate_up_again
    )
    grad_middle_norm, gain_two_grad = norm_two_back(grad_normed_two)
    grad_middle = scaled + grad_middle_norm
    (
        merged_again,
        adapt_merged_again,
        lift_query_again,
        lift_keyval_again,
        out_again,
        adapt_out_again,
        lift_out_again,
    ) = (
        lax.all_gather(merged_projection, ("fsdp", "seq"), axis=0, tiled=True),
        lax.all_gather(merged_adapter_in, ("fsdp", "seq"), axis=0, tiled=True),
        lax.all_gather(query_adapter_out, ("fsdp", "seq"), axis=0, tiled=True),
        lax.all_gather(keyval_adapter_out, ("fsdp", "seq"), axis=0, tiled=True),
        lax.all_gather(output_projection, ("fsdp", "seq"), axis=0, tiled=True),
        lax.all_gather(output_adapter_in, ("fsdp", "seq"), axis=0, tiled=True),
        lax.all_gather(output_adapter_out, ("fsdp", "seq"), axis=0, tiled=True),
    )
    grad_attn = grad_middle.astype(jnp.bfloat16)
    grad_lifted_out = times_transposed(grad_attn, lift_out_again).astype(jnp.bfloat16)
    grad_attention = (
        times_transposed(grad_attn, out_again) + times_transposed(grad_lifted_out, adapt_out_again)
    ).astype(jnp.bfloat16)
    grad_rows = grad_attention.reshape(row_total_count, HEAD_DIM)
    correction = jnp.sum(grad_rows.astype(jnp.float32) * attention_out, axis=1)

    def grad_step(grad_query, block_item):
        raw_scores, allowed = scores_of(block_item[1], block_item[0])
        soft_weights = jnp.where(allowed, jnp.exp(raw_scores - log_norm[:, None]), 0.0)
        grad_weights = times_transposed(grad_rows, block_item[2])
        grad_scores = (soft_weights * (grad_weights - correction[:, None])).astype(jnp.bfloat16)
        grad_query = grad_query + matmul(grad_scores, block_item[1]) * scale
        grad_key = transposed_times(grad_scores, query_rot) * scale
        grad_value = transposed_times(soft_weights.astype(jnp.bfloat16), grad_rows)
        return (grad_query, jnp.concatenate([grad_key, grad_value], axis=1))

    grad_query_rot, kv_terms = blockwise(
        grad_step,
        jnp.zeros((row_total_count, HEAD_DIM), jnp.float32),
        jnp.zeros((key_span, 2 * HEAD_DIM), jnp.float32),
    )
    kv_summed = lax.psum_scatter(
        kv_terms.reshape(length, 2 * HEAD_DIM), "seq", scatter_dimension=0, tiled=True
    )
    grad_keys = rotate_back(kv_summed[:, :HEAD_DIM], cosine_table, sine_table)
    grad_values = kv_summed[:, HEAD_DIM:]
    grad_query_pre = rotate_back(
        grad_query_rot.reshape(tokens, HEADS, HEAD_DIM),
        cosine_table[:, None, :],
        sine_table[:, None, :],
    ).reshape(tokens, query_width)
    grad_merged = jnp.concatenate([grad_query_pre, grad_keys, grad_values], axis=1).astype(
        jnp.bfloat16
    )
    grad_lifted = jnp.concatenate(
        [
            times_transposed(grad_merged[:, :query_width], lift_query_again),
            times_transposed(
                grad_merged[:, query_width : query_width + HEAD_DIM], lift_keyval_again[:RANK]
            ),
            times_transposed(grad_merged[:, query_width + HEAD_DIM :], lift_keyval_again[RANK:]),
        ],
        axis=1,
    ).astype(jnp.bfloat16)
    grad_normed_one = times_transposed(grad_merged, merged_again) + times_transposed(
        grad_lifted, adapt_merged_again
    )
    grad_hidden_norm, gain_one_grad = norm_one_back(grad_normed_one)
    hidden_grad = grad_middle + grad_hidden_norm
    gate_up_weight_grad = weight_gradient(second_in, grad_gate_up, gate_up_weight.shape[0])
    down_weight_grad = weight_gradient(inner, grad_branch, down_weight.shape[0])
    keyval_term = jnp.concatenate(
        [
            transposed_times(
                lifted[:, RANK : 2 * RANK], grad_merged[:, query_width : query_width + HEAD_DIM]
            ),
            transposed_times(lifted[:, 2 * RANK :], grad_merged[:, query_width + HEAD_DIM :]),
        ],
        axis=0,
    )
    gate_up_term = jnp.concatenate(
        [
            transposed_times(lifted_gate_up[:, :RANK], grad_gate_up[:, :FF]),
            transposed_times(lifted_gate_up[:, RANK:], grad_gate_up[:, FF:]),
        ],
        axis=0,
    )
    (
        gain_one_sum,
        merged_sum,
        merged_in_sum,
        query_out_sum,
        keyval_sum,
        out_proj_sum,
        out_in_sum,
        out_out_sum,
        gain_two_sum,
        gate_up_in_sum,
        gate_up_out_sum,
        down_in_sum,
        down_out_sum,
    ) = (
        lax.psum_scatter(gain_one_grad, ("fsdp", "seq"), scatter_dimension=0, tiled=True),
        lax.psum_scatter(
            transposed_times(first_in, grad_merged),
            ("fsdp", "seq"),
            scatter_dimension=0,
            tiled=True,
        ),
        lax.psum_scatter(
            transposed_times(first_in, grad_lifted),
            ("fsdp", "seq"),
            scatter_dimension=0,
            tiled=True,
        ),
        lax.psum_scatter(
            transposed_times(lifted[:, :RANK], grad_merged[:, :query_width]),
            ("fsdp", "seq"),
            scatter_dimension=0,
            tiled=True,
        ),
        lax.psum_scatter(keyval_term, ("fsdp", "seq"), scatter_dimension=0, tiled=True),
        lax.psum_scatter(
            transposed_times(attention_low, grad_attn),
            ("fsdp", "seq"),
            scatter_dimension=0,
            tiled=True,
        ),
        lax.psum_scatter(
            transposed_times(attention_low, grad_lifted_out),
            ("fsdp", "seq"),
            scatter_dimension=0,
            tiled=True,
        ),
        lax.psum_scatter(
            transposed_times(lifted_out, grad_attn),
            ("fsdp", "seq"),
            scatter_dimension=0,
            tiled=True,
        ),
        lax.psum_scatter(gain_two_grad, ("fsdp", "seq"), scatter_dimension=0, tiled=True),
        lax.psum_scatter(
            transposed_times(second_in, grad_lifted_gate_up),
            ("fsdp", "seq"),
            scatter_dimension=0,
            tiled=True,
        ),
        lax.psum_scatter(gate_up_term, ("fsdp", "seq"), scatter_dimension=0, tiled=True),
        lax.psum_scatter(
            transposed_times(inner, grad_lifted_down),
            ("fsdp", "seq"),
            scatter_dimension=0,
            tiled=True,
        ),
        lax.psum_scatter(
            transposed_times(lifted_down, grad_branch),
            ("fsdp", "seq"),
            scatter_dimension=0,
            tiled=True,
        ),
    )
    return (
        output.astype(jnp.bfloat16),
        hidden_grad.astype(jnp.bfloat16),
        gain_one_sum,
        merged_sum,
        merged_in_sum,
        query_out_sum,
        keyval_sum,
        out_proj_sum,
        out_in_sum,
        out_out_sum,
        gain_two_sum,
        gate_up_weight_grad,
        gate_up_in_sum,
        gate_up_out_sum,
        down_weight_grad,
        down_in_sum,
        down_out_sum,
    )


def solution(mesh):
    return jax.shard_map(
        per_device,
        mesh=mesh,
        in_specs=(
            P(("fsdp", "seq"), None),
            P(("fsdp", "seq"), None),
            P(("fsdp", "seq")),
            P(),
            P("fsdp"),
            P(("fsdp", "seq")),
            P(("fsdp", "seq"), None),
            P(("fsdp", "seq"), None),
            P(("fsdp", "seq"), None),
            P(("fsdp", "seq"), None),
            P(("fsdp", "seq"), None),
            P(("fsdp", "seq"), None),
            P(("fsdp", "seq"), None),
            P(("fsdp", "seq")),
            P(("fsdp", "seq"), None),
            P(("fsdp", "seq"), None),
            P(("fsdp", "seq"), None),
            P(("fsdp", "seq"), None),
            P(("fsdp", "seq"), None),
            P(("fsdp", "seq"), None),
        ),
        out_specs=(
            P(("fsdp", "seq"), None),
            P(("fsdp", "seq"), None),
            P(("fsdp", "seq")),
            P(("fsdp", "seq"), None),
            P(("fsdp", "seq"), None),
            P(("fsdp", "seq"), None),
            P(("fsdp", "seq"), None),
            P(("fsdp", "seq"), None),
            P(("fsdp", "seq"), None),
            P(("fsdp", "seq"), None),
            P(("fsdp", "seq")),
            P(("fsdp", "seq"), None),
            P(("fsdp", "seq"), None),
            P(("fsdp", "seq"), None),
            P(("fsdp", "seq"), None),
            P(("fsdp", "seq"), None),
            P(("fsdp", "seq"), None),
        ),
        check_vma=False,
    )
```

profile of v0, /device:TPU:0, one launch (start us, length us, event | category | flops | bytes accessed | tf_op | source)
XLA Modules:
  0.0 1735.9 jit_solution(4316568011635001110)
XLA Ops:
  11.2 42.0 %all-reduce.16 = (bf16[640]{0:T(1024)(128)(2,1)S(1)}, bf16[640]{0:T(1024)(128)(2,1)S(1)}) all-reduce(bf16[640]{0:T(1024)(128)(2,1)S(1)} %dynamic-update-slice, bf16[640]{0:T(1024)(128)(2,1)S(1)} %dynamic-update-slice.1), channel_id=1, replica_groups=mesh['fsdp'=2,'seq'=16] {'fsdp','seq'}, use_global_device_ids=true, to_apply=%add | all-reduce | flops 1280 | bytes 5120
  53.2 44.5 %all-gather.1 = bf16[32,20,768]{2,1,0:T(8,128)(2,1)S(1)} all-gather(bf16[1,20,768]{2,1,0:T(8,128)(2,1)} %bitcast.143), channel_id=1, replica_groups=mesh['fsdp'=2,'seq'=16] {'fsdp','seq'}, dimensions={0}, use_global_device_ids=true | all-gather | bytes 1013760 | tf_op jit(solution)/shard_map/all_gather | solution.py:106
  98.8 37.5 %all_gather.67 = bf16[512,256]{1,0:T(8,128)(2,1)S(1)} all-gather(bf16[16,256]{1,0:T(8,128)(2,1)S(1)} %copy-done.84), channel_id=1, replica_groups=mesh['fsdp'=2,'seq'=16] {'fsdp','seq'}, dimensions={0}, use_global_device_ids=true | all-gather | bytes 270336 | tf_op jit(solution)/shard_map/all_gather | solution.py:108
  138.2 2.7 reshape.215
  148.9 40.3 %all_gather.69 = bf16[256,1024]{1,0:T(8,128)(2,1)S(1)} all-gather(bf16[8,1024]{1,0:T(8,128)(2,1)} %param.40), channel_id=1, replica_groups=mesh['fsdp'=2,'seq'=16] {'fsdp','seq'}, dimensions={0}, use_global_device_ids=true | all-gather | bytes 540672 | tf_op jit(solution)/shard_map/all_gather | solution.py:107
  189.2 41.4 %all_gather.72 = bf16[1024,256]{1,0:T(8,128)(2,1)} all-gather(bf16[32,256]{1,0:T(8,128)(2,1)} %param.43), channel_id=1, replica_groups=mesh['fsdp'=2,'seq'=16] {'fsdp','seq'}, dimensions={0}, use_global_device_ids=true | all-gather | bytes 540672 | tf_op jit(solution)/shard_map/all_gather | solution.py:110
  230.6 42.3 %all_gather.73 = bf16[256,640]{1,0:T(8,128)(2,1)} all-gather(bf16[8,640]{1,0:T(8,128)(2,1)} %param.44), channel_id=1, replica_groups=mesh['fsdp'=2,'seq'=16] {'fsdp','seq'}, dimensions={0}, use_global_device_ids=true | all-gather | bytes 337920 | tf_op jit(solution)/shard_map/all_gather | solution.py:111
  272.9 38.0 %all_gather.80 = bf16[256,640]{1,0:T(8,128)(2,1)S(1)} all-gather(bf16[8,640]{1,0:T(8,128)(2,1)} %param.51), channel_id=1, replica_groups=mesh['fsdp'=2,'seq'=16] {'fsdp','seq'}, dimensions={0}, use_global_device_ids=true | all-gather | bytes 337920 | tf_op jit(solution)/shard_map/all_gather | solution.py:213
  310.9 40.7 %all-gather.3 = bf16[32,20,512]{2,1,0:T(8,128)(2,1)S(1)} all-gather(bf16[1,20,512]{2,1,0:T(8,128)(2,1)S(1)} %bitcast.144), channel_id=1, replica_groups=mesh['fsdp'=2,'seq'=16] {'fsdp','seq'}, dimensions={0}, use_global_device_ids=true | all-gather | bytes 675840 | tf_op jit(solution)/shard_map/all_gather | solution.py:209
  355.5 2.6 convolution_add_fusion.4
  358.1 2.7 reshape.203
  362.4 4.1 convolution_add_fusion
  366.4 18.9 %while.43 = (s32[]{:T(128)}, f32[1024]{0:T(1024)S(1)}, f32[1024]{0:T(1024)S(1)}, s32[8]{0:T(128)S(1)}, s32[]{:T(128)}, /*index=5*/s32[]{:T(128)}, bf16[8,512,256...) while((s32[]{:T(128)}, f32[1024]{0:T(1024)S(1)}, f32[1024]{0:T(1024)S(1)}, ...), condition=%wide.region_6.7_spmd.clone, body=%wide.region_1.6_spmd.clone.sunk | while | flops 272118272 | bytes 5072695 | solution.py:169
  368.4 3.3 conditional.9
  386.1 19.3 %while.44 = (s32[]{:T(128)}, f32[1024,256]{1,0:T(8,128)S(1)}, s32[8]{0:T(128)S(1)}, s32[]{:T(128)}, s32[]{:T(128)}, /*index=5*/bf16[8,512,256]{2,1,0:T(8,128)(2,...) while((s32[]{:T(128)}, f32[1024,256]{1,0:T(8,128)S(1)}, ...), condition=%wide.region_10.11_spmd.clone, body=%wide.region_7.10_spmd.clone.sunk | while | flops 540289536 | bytes 3189031 | solution.py:169
  388.0 3.7 conditional.10
  389.4 2.4 fusion.17
  410.7 2.2 multiply_reduce_fusion.3
  414.2 8.1 reshape.219
  422.2 6.3 fusion.148
  428.6 32.0 %all-gather.19.cloned.1.call-done = bf16[512,2048]{1,0:T(8,128)(2,1)} async-done(((bf16[16,2048]{1,0:T(8,128)(2,1)}), bf16[512,2048]{1,0:T(8,128)(2,1)}) %all-gather.19.cloned.1.call-update) | async-done | bytes 2097168 | tf_op jit(solution)/shard_map/all_gather | solution.py:210
  460.6 2.5 convolution_add_fusion.1
  463.1 4.8 fusion.57
  482.3 36.4 %while.45 = (s32[]{:T(128)}, f32[1024,256]{1,0:T(8,128)}, f32[8,512,512]{2,1,0:T(8,128)}, s32[8]{0:T(128)S(1)}, s32[]{:T(128)}, /*index=5*/s32[]{:T(128)}, bf16[...) while((s32[]{:T(128)}, f32[1024,256]{1,0:T(8,128)}, ...), condition=%wide.region_18.19_spmd.clone, body=%wide.region_15.18_spmd.clone.sunk | while | flops 1347824128 | bytes 21806608 | solution.py:169
  484.4 8.4 conditional.11
  488.9 2.8 fusion.37
  521.0 2.3 fusion.109
  526.8 2.1 fusion.152
  532.0 2.6 pad_maximum_fusion
  535.5 3.4 fusion.132
  540.6 2.7 fusion.86
  545.1 5.5 fusion.58
  550.5 70.3 %all-reduce.20.cloned.1.call-done = (f32[256,640]{1,0:T(8,128)}, f32[256,640]{1,0:T(8,128)}) async-done(((f32[256,640]{1,0:T(8,128)}, f32[256,640]{1,0:T(8,128)}), (f32[256,640]{1,0:T(8,128)}, f32[256,640]{1,0:T(8,128)})) %all-reduce.20.cloned.1.call-update) | async-done | bytes 1310736
  622.2 105.0 %reduce-scatter.17.cloned.1.call-done = f32[256,512]{1,0:T(8,128)} async-done(((f32[4096,512]{1,0:T(8,128)}), f32[256,512]{1,0:T(8,128)}) %reduce-scatter.17.cloned.1.call-update) | async-done | bytes 524304 | tf_op jit(solution)/shard_map/reduce_scatter | solution.py:305
  733.1 2.6 fusion.89
  735.7 241.5 %fusion.141 = (f32[24,1536]{1,0:T(8,128)S(1)}, f32[24,768]{1,0:T(8,128)}, f32[24,4096]{1,0:T(8,128)S(1)}, f32[24,512]{1,0:T(8,128)}) fusion(f32[640,1536]{1,0:T(8,128)} %fusion.89, f32[640,768]{1,0:T(8,128)} %fusion.87, f32[640,4096]{1,0:T(8,128)} %fusion.58, f32[640,512]{1,0:T(8,128)S(1)} %copy-done.17), kind=kCustom, calls=%all-reduce-scatter.4 | all-reduce-scatter fusion | flops 5308417 | bytes 18358272
  978.1 10.0 collective-permute-start.22
  988.1 4.1 collective-permute-start.5
  993.0 3.5 collective-permute-start.11
  996.5 4.1 collective-permute-start.23
  1005.6 3.3 collective-permute-start.21
  1009.0 3.9 collective-permute-start.20
  1014.8 2.6 collective-permute-start.18
  1021.5 2.5 collective-permute-start.9
  1024.0 2.5 collective-permute-start.8
  1026.6 3.1 collective-permute-start.7
  1034.5 2.2 collective-permute-start.3
  1036.8 2.7 collective-permute-start.2
  1039.4 2.5 collective-permute-start.1
  1041.9 5.9 collective-permute-start
  1048.8 38.1 %all-reduce.14 = (f32[640]{0:T(1024)S(1)}, f32[640]{0:T(1024)S(1)}) all-reduce(f32[640]{0:T(1024)S(1)} %get-tuple-element.639, f32[640]{0:T(1024)S(1)} %copy-done.75), channel_id=3, replica_groups=mesh['fsdp'=2,'seq'=16] {'fsdp','seq'}, use_global_device_ids=true, to_apply=%region_22.23.clone | all-reduce | flops 1280 | bytes 10240
  1088.1 4.5 concatenate.63
  1092.7 2.8 collective-permute-start.16
  1095.5 3.4 collective-permute-start.15
  1098.8 4.1 collective-permute-start.14
  1103.0 4.4 collective-permute-start.13
  1110.0 4.0 concatenate.61
  1117.3 3.6 collective-permute-done.13
  1120.8 11.3 concatenate.62
  1132.9 36.2 %reduce-scatter.31.cloned.1.call-done = f32[64,256]{1,0:T(8,128)} async-done(((f32[2048,256]{1,0:T(8,128)}), f32[64,256]{1,0:T(8,128)}) %reduce-scatter.31.cloned.1.call-update) | async-done | bytes 65552 | tf_op jit(solution)/shard_map/reduce_scatter | solution.py:412
  1169.1 140.8 %reduce-scatter.23.cloned.1.call-done = f32[32,640]{1,0:T(8,128)} async-done(((f32[1024,640]{1,0:T(8,128)}), f32[32,640]{1,0:T(8,128)}) %reduce-scatter.23.cloned.1.call-update) | async-done | bytes 81936 | tf_op jit(solution)/shard_map/reduce_scatter | solution.py:386
  1309.9 140.9 %reduce-scatter.27.cloned.1.call-done = f32[16,2048]{1,0:T(8,128)} async-done(((f32[512,2048]{1,0:T(8,128)}), f32[16,2048]{1,0:T(8,128)}) %reduce-scatter.27.cloned.1.call-update) | async-done | bytes 131088 | tf_op jit(solution)/shard_map/reduce_scatter | solution.py:411
  1450.8 143.9 %reduce-scatter.29.cloned.1.call-done = f32[64,640]{1,0:T(8,128)} async-done(((f32[2048,640]{1,0:T(8,128)}), f32[64,640]{1,0:T(8,128)}) %reduce-scatter.29.cloned.1.call-update) | async-done | bytes 163856 | tf_op jit(solution)/shard_map/reduce_scatter | solution.py:67
  1594.8 134.3 %reduce-scatter.21.cloned.1.call-done = f32[16,256]{1,0:T(8,128)} async-done(((f32[512,256]{1,0:T(8,128)}), f32[16,256]{1,0:T(8,128)}) %reduce-scatter.21.cloned.1.call-update) | async-done | bytes 16400 | tf_op jit(solution)/shard_map/reduce_scatter | solution.py:385
  (503 shorter events, 124.5 us)
Async XLA Ops:
  7.2 91.6 %copy-start.84 = (bf16[16,256]{1,0:T(8,128)(2,1)S(1)}, bf16[16,256]{1,0:T(8,128)(2,1)}, u32[]{:S(2)}) copy-start(bf16[16,256]{1,0:T(8,128)(2,1)} %param.41) | copy-start | bytes 24580
  7.2 129.1 %copy-start.6 = (bf16[256,640]{1,0:T(8,128)(2,1)S(1)}, bf16[256,640]{1,0:T(8,128)(2,1)}, u32[]{:S(2)}) copy-start(bf16[256,640]{1,0:T(8,128)(2,1)} %param.32) | copy-start | bytes 983044
  7.2 131.0 %all-gather.25.cloned.1.call-start = ((), (), s32[]{:S(2)}) async-start(), calls=%async_computation.22 | async-start | bytes 2433024 | tf_op jit(solution)/shard_map/all_gather | solution.py:105
  7.9 345.8 %all-gather.23.cloned.1.call-start = ((), (), s32[]{:S(2)}) async-start(), calls=%async_computation.13 | async-start | bytes 1081344 | tf_op jit(solution)/shard_map/all_gather | solution.py:212
  8.7 353.7 %all-gather.21.cloned.1.call-start = ((), (), s32[]{:S(2)}) async-start(), calls=%async_computation.12 | async-start | bytes 2703360 | tf_op jit(solution)/shard_map/all_gather | solution.py:211
  9.4 357.0 %all-gather.13.cloned.1.call-start = ((), (), s32[]{:S(2)}) async-start(), calls=%async_computation.8 | async-start | bytes 2228224 | tf_op jit(solution)/shard_map/all_gather | solution.py:140
  98.8 43.2 %copy-start.87 = (f32[128]{0:T(128)}, f32[128]{0:T(128)S(1)}, u32[]{:S(2)}) copy-start(f32[128]{0:T(128)S(1)} %multiply_power_fusion) | copy-start | bytes 1540
  143.0 217.8 %copy-start.41 = (f32[256,128]{1,0:T(8,128)}, f32[256,128]{1,0:T(8,128)S(1)}, u32[]{:S(2)}) copy-start(f32[256,128]{1,0:T(8,128)S(1)} %get-tuple-element.734) | copy-start | bytes 393220
  143.0 217.8 %copy-start.43 = (f32[256,128]{1,0:T(8,128)}, f32[256,128]{1,0:T(8,128)S(1)}, u32[]{:S(2)}) copy-start(f32[256,128]{1,0:T(8,128)S(1)} %get-tuple-element.735) | copy-start | bytes 393220
  143.0 168.0 %copy-start.72 = (bf16[20,512]{1,0:T(8,128)(2,1)S(1)}, bf16[20,512]{1,0:T(8,128)(2,1)}, u32[]{:S(2)}) copy-start(bf16[20,512]{1,0:T(8,128)(2,1)} %param.47) | copy-start | bytes 61444
  143.7 242.3 %all-gather.15.cloned.1.call-start = ((), (), s32[]{:S(2)}) async-start(), calls=%async_computation.9 | async-start | bytes 2228224 | tf_op jit(solution)/shard_map/all_gather | solution.py:141
  145.6 265.1 %all-gather.17.cloned.1.call-start = ((), (), s32[]{:S(2)}) async-start(), calls=%async_computation.10 | async-start | bytes 1351680 | tf_op jit(solution)/shard_map/all_gather | solution.py:109
  146.2 268.0 %all-gather.27.cloned.1.call-start = ((), (), s32[]{:S(2)}) async-start(), calls=%async_computation.23 | async-start | bytes 6488064 | tf_op jit(solution)/shard_map/all_gather | solution.py:208
  146.9 205.7 %copy-start.89 = (s32[256]{0:T(256)S(1)}, s32[256]{0:T(256)}, u32[]{:S(2)}) copy-start(s32[256]{0:T(256)} %param.34) | copy-start | bytes 3076
  146.9 205.7 %copy-start.90 = (f32[16]{0:T(128)S(1)}, f32[16]{0:T(128)}, u32[]{:S(2)}) copy-start(f32[16]{0:T(128)} %param.35) | copy-start | bytes 196
  147.0 205.8 %copy-start.19 = (bf16[256,640]{1,0:T(8,128)(2,1)S(1)}, bf16[256,640]{1,0:T(8,128)(2,1)}, u32[]{:S(2)}) copy-start(bf16[256,640]{1,0:T(8,128)(2,1)} %param.33) | copy-start | bytes 983044
  147.0 313.6 %all-gather.19.cloned.1.call-start = ((), (), s32[]{:S(2)}) async-start(), calls=%async_computation.11 | async-start | bytes 2162688 | tf_op jit(solution)/shard_map/all_gather | solution.py:210
  147.7 473.2 %all-reduce.20.cloned.1.call-start = ((), (), s32[]{:S(2)}) async-start(), calls=%async_computation.24 | async-start | bytes 2621440
  189.2 166.3 %copy-start.23 = (bf16[256,1024]{1,0:T(8,128)(2,1)}, bf16[256,1024]{1,0:T(8,128)(2,1)S(1)}, u32[]{:S(2)}) copy-start(bf16[256,1024]{1,0:T(8,128)(2,1)S(1)} %all_gather.69) | copy-start | bytes 1572868
  413.0 59.9 %copy-start.2 = (f32[256,640]{1,0:T(8,128)}, f32[256,640]{1,0:T(8,128)S(1)}, u32[]{:S(2)}) copy-start(f32[256,640]{1,0:T(8,128)S(1)} %get-tuple-element.739) | copy-start | bytes 1966084
  414.1 46.5 %copy-start.35 = (bf16[256,512]{1,0:T(8,128)(2,1)}, bf16[256,512]{1,0:T(8,128)(2,1)S(1)}, u32[]{:S(2)}) copy-start(bf16[256,512]{1,0:T(8,128)(2,1)S(1)} %convolution_convert_fusion.1) | copy-start | bytes 786436
  481.2 246.0 %reduce-scatter.17.cloned.1.call-start = ((), (), s32[]{:S(2)}) async-start(), calls=%async_computation.14 | async-start | bytes 8912896 | tf_op jit(solution)/shard_map/reduce_scatter | solution.py:305
  518.7 614.2 %reduce-scatter.19.cloned.1.call-start = ((), (), s32[]{:S(2)}) async-start(), calls=%async_computation.15 | async-start | bytes 1081344 | tf_op jit(solution)/shard_map/reduce_scatter | solution.py:379
  523.3 609.6 %reduce-scatter.25.cloned.1.call-start = ((), (), s32[]{:S(2)}) async-start(), calls=%async_computation.18 | async-start | bytes 1081344 | tf_op jit(solution)/shard_map/reduce_scatter | solution.py:392
  524.8 644.3 %reduce-scatter.31.cloned.1.call-start = ((), (), s32[]{:S(2)}) async-start(), calls=%async_computation.21 | async-start | bytes 2162688 | tf_op jit(solution)/shard_map/reduce_scatter | solution.py:412
  526.7 783.2 %reduce-scatter.23.cloned.1.call-start = ((), (), s32[]{:S(2)}) async-start(), calls=%async_computation.17 | async-start | bytes 2703360 | tf_op jit(solution)/shard_map/reduce_scatter | solution.py:386
  528.9 921.9 %reduce-scatter.27.cloned.1.call-start = ((), (), s32[]{:S(2)}) async-start(), calls=%async_computation.19 | async-start | bytes 4325376 | tf_op jit(solution)/shard_map/reduce_scatter | solution.py:411
  534.6 1060.2 %reduce-scatter.29.cloned.1.call-start = ((), (), s32[]{:S(2)}) async-start(), calls=%async_computation.20 | async-start | bytes 5406720 | tf_op jit(solution)/shard_map/reduce_scatter | solution.py:67
  539.0 1190.1 %reduce-scatter.21.cloned.1.call-start = ((), (), s32[]{:S(2)}) async-start(), calls=%async_computation.16 | async-start | bytes 540672 | tf_op jit(solution)/shard_map/reduce_scatter | solution.py:385
  545.1 183.1 %copy-start.86 = (f32[256]{0:T(256)S(1)}, f32[256]{0:T(256)}, u32[]{:S(2)}) copy-start(f32[256]{0:T(256)} %copy-done.85) | copy-start | bytes 3076
  545.1 183.1 %copy-start.88 = (f32[128]{0:T(128)S(1)}, f32[128]{0:T(128)}, u32[]{:S(2)}) copy-start(f32[128]{0:T(128)} %copy-done.87) | copy-start | bytes 1540
  545.1 184.7 %copy-start.34 = (bf16[512,256]{1,0:T(8,128)(2,1)S(1)}, bf16[512,256]{1,0:T(8,128)(2,1)}, u32[]{:S(2)}) copy-start(bf16[512,256]{1,0:T(8,128)(2,1)} %copy-done.33) | copy-start | bytes 786436
  735.7 264.9 %copy-start.38 = (bf16[256,768]{1,0:T(8,128)(2,1)S(1)}, bf16[256,768]{1,0:T(8,128)(2,1)}, u32[]{:S(2)}) copy-start(bf16[256,768]{1,0:T(8,128)(2,1)} %copy-done.37) | copy-start | bytes 1179652
  978.1 39.3 %collective-permute-start.22 = (f32[24,512]{1,0:T(8,128)}, f32[24,512]{1,0:T(8,128)S(1)}, u32[]{:S(2)}, u32[]{:S(2)}) collective-permute-start(f32[24,512]{1,0:T(8,128)} %get-tuple-element.718), channel_id=1, source_target_pairs={{0,5},{1,6},{2,7},{3,8},{4,9},{5,10},{6,11},{7,12},{8,13},{9,14},{... | collective-permute-start | bytes 147464
  988.1 26.7 %collective-permute-start.5 = (f32[4,1536]{1,0:T(4,128)S(1)}, f32[4,1536]{1,0:T(4,128)S(1)}, u32[]{:S(2)}, u32[]{:S(2)}) collective-permute-start(f32[4,1536]{1,0:T(4,128)S(1)} %slice.145), channel_id=1, source_target_pairs={{0,6},{1,7},{2,8},{3,9},{4,10},{5,11},{6,12},{7,13},{8,14},{9,15},... | collective-permute-start | bytes 73736
  993.0 19.9 %collective-permute-start.11 = (f32[4,768]{1,0:T(4,128)S(1)}, f32[4,768]{1,0:T(4,128)S(1)}, u32[]{:S(2)}, u32[]{:S(2)}) collective-permute-start(f32[4,768]{1,0:T(4,128)S(1)} %slice.146), channel_id=1, source_target_pairs={{0,6},{1,7},{2,8},{3,9},{4,10},{5,11},{6,12},{7,13},{8,14},{9,15},... | collective-permute-start | bytes 36872
  996.5 12.4 collective-permute-start.23
  1005.4 43.4 %copy-start.75 = (f32[640]{0:T(1024)S(1)}, f32[640]{0:T(1024)}, u32[]{:S(2)}) copy-start(f32[640]{0:T(1024)} %get-tuple-element.637) | copy-start | bytes 7684
  1005.6 13.9 collective-permute-start.21
  1009.0 12.5 collective-permute-start.20
  1012.9 11.1 collective-permute-start.19
  1014.8 11.8 collective-permute-start.18
  1017.5 12.2 collective-permute-start.17
  1019.5 13.2 collective-permute-start.10
  1021.5 13.0 collective-permute-start.9
  1024.0 12.7 collective-permute-start.8
  1026.6 12.8 collective-permute-start.7
  1029.7 12.2 collective-permute-start.6
  1032.6 55.5 %copy-start.83 = (f32[4,512]{1,0:T(4,128)S(1)}, f32[4,512]{1,0:T(4,128)}, u32[]{:S(2)}) copy-start(f32[4,512]{1,0:T(4,128)} %copy-done.82) | copy-start | bytes 24580
  1032.6 77.4 %copy-start.77 = (f32[4,768]{1,0:T(4,128)S(1)}, f32[4,768]{1,0:T(4,128)}, u32[]{:S(2)}) copy-start(f32[4,768]{1,0:T(4,128)} %copy-done.76) | copy-start | bytes 36868
  1032.6 82.0 %copy-start.71 = (f32[4,1536]{1,0:T(4,128)S(1)}, f32[4,1536]{1,0:T(4,128)}, u32[]{:S(2)}) copy-start(f32[4,1536]{1,0:T(4,128)} %copy-done.70) | copy-start | bytes 73732
  1032.7 60.0 %collective-permute-start.4 = (f32[24,1536]{1,0:T(8,128)S(1)}, f32[24,1536]{1,0:T(8,128)S(1)}, u32[]{:S(2)}, u32[]{:S(2)}) collective-permute-start(f32[24,1536]{1,0:T(8,128)S(1)} %get-tuple-element.715), channel_id=1, source_target_pairs={{0,5},{1,6},{2,7},{3,8},{4,9},{5,10},{6,11},{7,12},{8,13},{9,14},{... | collective-permute-start | bytes 442376
  1034.5 58.2 %copy-start.64 = (f32[24,768]{1,0:T(8,128)}, f32[24,768]{1,0:T(8,128)S(1)}, u32[]{:S(2)}) copy-start(f32[24,768]{1,0:T(8,128)S(1)} %collective-permute-done.9) | copy-start | bytes 221188
  1034.5 61.0 %collective-permute-start.3 = (f32[24,1536]{1,0:T(8,128)S(1)}, f32[24,1536]{1,0:T(8,128)S(1)}, u32[]{:S(2)}, u32[]{:S(2)}) collective-permute-start(f32[24,1536]{1,0:T(8,128)S(1)} %get-tuple-element.715), channel_id=1, source_target_pairs={{0,4},{1,5},{2,6},{3,7},{4,8},{5,9},{6,10},{7,11},{8,12},{9,13},{1... | collective-permute-start | bytes 442376
  1036.7 55.9 %copy-start.65 = (f32[24,768]{1,0:T(8,128)}, f32[24,768]{1,0:T(8,128)S(1)}, u32[]{:S(2)}) copy-start(f32[24,768]{1,0:T(8,128)S(1)} %collective-permute-done.8) | copy-start | bytes 221188
  1036.7 73.3 %copy-start.63 = (f32[24,768]{1,0:T(8,128)S(1)}, f32[24,768]{1,0:T(8,128)}, u32[]{:S(2)}) copy-start(f32[24,768]{1,0:T(8,128)} %copy-done.62) | copy-start | bytes 221188
  1036.8 62.1 %collective-permute-start.2 = (f32[24,1536]{1,0:T(8,128)S(1)}, f32[24,1536]{1,0:T(8,128)S(1)}, u32[]{:S(2)}, u32[]{:S(2)}) collective-permute-start(f32[24,1536]{1,0:T(8,128)S(1)} %get-tuple-element.715), channel_id=1, source_target_pairs={{0,3},{1,4},{2,5},{3,6},{4,7},{5,8},{6,9},{7,10},{8,11},{9,12},{10... | collective-permute-start | bytes 442376
  1039.4 63.5 %collective-permute-start.1 = (f32[24,1536]{1,0:T(8,128)S(1)}, f32[24,1536]{1,0:T(8,128)S(1)}, u32[]{:S(2)}, u32[]{:S(2)}) collective-permute-start(f32[24,1536]{1,0:T(8,128)S(1)} %get-tuple-element.715), channel_id=1, source_target_pairs={{0,2},{1,3},{2,4},{3,5},{4,6},{5,7},{6,8},{7,9},{8,10},{9,11},{10,... | collective-permute-start | bytes 442376
  1041.9 65.4 %collective-permute-start = (f32[24,1536]{1,0:T(8,128)S(1)}, f32[24,1536]{1,0:T(8,128)S(1)}, u32[]{:S(2)}, u32[]{:S(2)}) collective-permute-start(f32[24,1536]{1,0:T(8,128)S(1)} %get-tuple-element.715), channel_id=1, source_target_pairs={{0,1},{1,2},{2,3},{3,4},{4,5},{5,6},{6,7},{7,8},{8,9},{9,10},{10,1... | collective-permute-start | bytes 442376
  1092.7 24.6 %collective-permute-start.16 = (f32[24,4096]{1,0:T(8,128)S(1)}, f32[24,4096]{1,0:T(8,128)S(1)}, u32[]{:S(2)}, u32[]{:S(2)}) collective-permute-start(f32[24,4096]{1,0:T(8,128)S(1)} %get-tuple-element.717), channel_id=1, source_target_pairs={{0,5},{1,6},{2,7},{3,8},{4,9},{5,10},{6,11},{7,12},{8,13},{9,14},{... | collective-permute-start | bytes 1179656
  1095.5 21.8 %collective-permute-start.15 = (f32[24,4096]{1,0:T(8,128)S(1)}, f32[24,4096]{1,0:T(8,128)}, u32[]{:S(2)}, u32[]{:S(2)}) collective-permute-start(f32[24,4096]{1,0:T(8,128)S(1)} %get-tuple-element.717), channel_id=1, source_target_pairs={{0,4},{1,5},{2,6},{3,7},{4,8},{5,9},{6,10},{7,11},{8,12},{9,13},{1... | collective-permute-start | bytes 1179656
  1098.8 18.5 %collective-permute-start.14 = (f32[24,4096]{1,0:T(8,128)S(1)}, f32[24,4096]{1,0:T(8,128)}, u32[]{:S(2)}, u32[]{:S(2)}) collective-permute-start(f32[24,4096]{1,0:T(8,128)S(1)} %get-tuple-element.717), channel_id=1, source_target_pairs={{0,3},{1,4},{2,5},{3,6},{4,7},{5,8},{6,9},{7,10},{8,11},{9,12},{10... | collective-permute-start | bytes 1179656
  1103.0 17.9 %collective-permute-start.13 = (f32[24,4096]{1,0:T(8,128)S(1)}, f32[24,4096]{1,0:T(8,128)}, u32[]{:S(2)}, u32[]{:S(2)}) collective-permute-start(f32[24,4096]{1,0:T(8,128)S(1)} %get-tuple-element.717), channel_id=1, source_target_pairs={{0,2},{1,3},{2,4},{3,5},{4,6},{5,7},{6,8},{7,9},{8,10},{9,11},{10,... | collective-permute-start | bytes 1179656
  1107.3 13.5 collective-permute-start.12
  (81 other events, 494.2 us)
Sparse Core Ops, SparseCore 0:
  10.9 61.6 all-gather.24
  75.5 52.4 all-gather.22
  130.9 57.1 all-gather.20
  190.7 40.6 all-gather.12
  234.0 41.4 all-gather.14
  278.2 53.6 all-gather.16
  334.7 68.0 all-gather.26
  405.7 54.8 all-gather.18
  481.3 139.5 all-reduce.19
  624.8 102.3 reduce-scatter.16
  730.0 144.7 reduce-scatter.18
  877.5 148.1 reduce-scatter.24
  1028.5 140.5 reduce-scatter.30
  1171.8 138.0 reduce-scatter.22
  1312.6 138.1 reduce-scatter.26
  1453.5 141.1 reduce-scatter.28
  1597.4 131.6 reduce-scatter.20
where the time goes:
time: 1750 us; the launch traced here: 1740 us
  waiting for transfers between devices  811 us (46%)
  blocking collectives  606 us (35%)
  matrix products  86.2 us (5%)
  local copies, waits for them, and re-layouts  83.6 us (5%)
  starting transfers between devices  80.2 us (5%)
  loops' own time  33 us (2%)
  other arithmetic  18.6 us (1%)
    unnamed x3, blocking collectives  322 us
    reduce_scatter x1, waiting for transfers between devices, weight_gradient(): lax.psum_scatter(transposed_times(lax.slice_in_dim(activations, 0, shard_...  144 us
    reduce_scatter x1, waiting for transfers between devices, per_device(): lax.psum_scatter(gate_up_term, ('fsdp', 'seq'), scatter_dimension=0, tile...  141 us
    reduce_scatter x1, waiting for transfers between devices, per_device(): lax.psum_scatter(transposed_times(attention_low, grad_attn), ('fsdp', 'se...  141 us
    reduce_scatter x1, waiting for transfers between devices, per_device(): lax.psum_scatter(keyval_term, ('fsdp', 'seq'), scatter_dimension=0, tiled...  134 us
    reduce_scatter x1, waiting for transfers between devices, per_device(): lax.psum_scatter(kv_terms.reshape(length, 2 * HEAD_DIM), 'seq', scatter_d...  105 us
    unnamed x25, starting transfers between devices  79.3 us
    unnamed x42, waiting for transfers between devices  78.1 us
  transfers between devices with their start and end apart: 41, of which 9 were waited for; matrix products, arithmetic and copies ran while one was open for 23% of the time, Pallas kernels for 0%

commit v1 on v0

v1 whole, which is shorter than its diff:
```python
from functools import partial

import jax
import jax.numpy as jnp
from jax import lax
from jax.experimental import pallas as pl
from jax.experimental.pallas import tpu as pltpu
from jax.sharding import PartitionSpec as P

HEADS = 4
HEAD_DIM = 256
FF = 2048
RANK = 256
DATASETS = 16
EPSILON = 1e-06
MESH = pl.DeviceIdType.MESH
VMEM_LIMIT = 60 * 1024 * 1024
AXES = ("fsdp", "seq")
BF16 = jnp.bfloat16
F32 = jnp.float32


def rms_scale(values, gain_vector):
    inverse = lax.rsqrt(jnp.mean(values * values, axis=-1, keepdims=True) + EPSILON)
    return values * inverse * gain_vector


def rotary_tables(positions):
    half_width = HEAD_DIM // 2
    inverse = 10000.0 ** (-2.0 * jnp.arange(half_width, dtype=F32) / HEAD_DIM)
    angles = positions.astype(F32)[:, None] * inverse[None, :]
    return (jnp.cos(angles), jnp.sin(angles))


def rotate(values, cosine_table, sine_table):
    half_width = values.shape[-1] // 2
    first = values[..., :half_width]
    second = values[..., half_width:]
    return jnp.concatenate(
        [first * cosine_table - second * sine_table, second * cosine_table + first * sine_table],
        axis=-1,
    )


def rotate_heads(values, cosine_table, sine_table):
    parts = [
        rotate(values[:, h * HEAD_DIM : (h + 1) * HEAD_DIM], cosine_table, sine_table)
        for h in range(HEADS)
    ]
    return jnp.concatenate(parts, axis=1)


def matmul(left_side, right_side):
    return jnp.dot(left_side, right_side, preferred_element_type=F32)


def times_transposed(left_side, right_side):
    return lax.dot_general(
        left_side, right_side, (((1,), (1,)), ((), ())), preferred_element_type=F32
    )


def transposed_times(left_side, right_side, out=F32):
    return lax.dot_general(
        left_side, right_side, (((0,), (0,)), ((), ())), preferred_element_type=F32
    ).astype(out)


def padded_rows(rows):
    return -(-rows // 8) * 8


def pad_shard(shard):
    rows = shard.shape[0]
    return jnp.pad(shard, ((0, padded_rows(rows) - rows), (0, 0)))


def selection(rows, count):
    wide = padded_rows(rows)
    source = lax.broadcasted_iota(jnp.int32, (count * rows, count * wide), 0)
    target = lax.broadcasted_iota(jnp.int32, (count * rows, count * wide), 1)
    inside = target % wide
    return ((source == target // wide * rows + inside) & (inside < rows)).astype(BF16)


def spread(values, rows):
    if padded_rows(rows) == rows:
        return values
    return matmul(values, selection(rows, values.shape[1] // rows)).astype(BF16)


def collect(values, rows):
    wide = padded_rows(rows)
    if wide == rows:
        return values
    chosen = selection(rows, values.shape[1] // wide)
    first = values.astype(BF16)
    rest = values - first.astype(F32)
    second = rest.astype(BF16)
    third = (rest - second.astype(F32)).astype(BF16)
    return (
        times_transposed(first, chosen)
        + times_transposed(second, chosen)
        + times_transposed(third, chosen)
    )


def place(groups):
    f = lax.axis_index("fsdp")
    s = lax.axis_index("seq")
    c = lax.rem(s, 2)
    y = lax.rem(s // 2, 2)
    z = s // 4
    return f, z, y, c


def device(f, z, y, c):
    return (f, (z * 2 + y) * 2 + c)


def greet(groups, both):
    f, z, y, c = place(groups)
    barrier = pltpu.get_barrier_semaphore()
    peers = [device(f, z, y, 1 - c), device(f, z, 1 - y, c)]
    if both:
        peers.append(device(1 - f, z, y, c))
    for d in range(1, groups):
        peers.append(device(f, lax.rem(z + d, groups), y, c))
    for peer in peers:
        pl.semaphore_signal(barrier, inc=1, device_id=peer, device_id_type=MESH)
    pl.semaphore_wait(barrier, len(peers))


def gather_kernel(groups, orders, *refs):
    count = len(orders)
    ins, outs = refs[:count], refs[count : 2 * count]
    send, recv, local = refs[2 * count :]
    f, z, y, c = place(groups)
    greet(groups, True)

    def remote(src, dst, a, slot, peer):
        return pltpu.make_async_remote_copy(
            src_ref=src,
            dst_ref=dst,
            send_sem=send.at[a, slot],
            recv_sem=recv.at[a, slot],
            device_id=peer,
            device_id_type=MESH,
        )

    core = device(f, z, y, 1 - c)
    across = {"y": device(f, z, 1 - y, c), "x": device(1 - f, z, y, c)}
    started = []

    def start(copy):
        copy.start()
        started.append(copy)

    for a in range(count):
        pltpu.make_async_copy(ins[a], outs[a].at[f, z, y, c], local.at[a]).start()
        for d in range(1, groups):
            start(
                remote(
                    ins[a],
                    outs[a].at[f, z, y, c],
                    a,
                    d,
                    device(f, lax.rem(z + d, groups), y, c),
                )
            )
    for a in range(count):
        pltpu.make_async_copy(ins[a], outs[a].at[f, z, y, c], local.at[a]).wait()
        for d in range(1, groups):
            block = outs[a].at[f, lax.rem(z + groups - d, groups), y, c]
            remote(block, block, a, d, core).wait_recv()
        mine = outs[a].at[f, :, y, c]
        start(remote(mine, mine, a, 0, across[orders[a][0]]))
        start(remote(mine, mine, a, groups, core))
    for a in range(count):
        if orders[a] == "yx":
            got = outs[a].at[f, :, 1 - y, c]
            mine = outs[a].at[f, :, :, c]
        else:
            got = outs[a].at[1 - f, :, y, c]
            mine = outs[a].at[:, :, y, c]
        remote(got, got, a, 0, core).wait_recv()
        start(remote(mine, mine, a, groups + 1, across[orders[a][1]]))
        start(remote(got, got, a, groups + 2, core))
    for a in range(count):
        if orders[a] == "yx":
            got = outs[a].at[1 - f, :, :, c]
        else:
            got = outs[a].at[:, :, 1 - y, c]
        remote(got, got, a, groups + 1, core).wait_recv()
        start(remote(got, got, a, groups + 3, core))
    for a in range(count):
        other = 1 - c
        block = outs[a].at[f, :, y, other]
        remote(block, block, a, groups, core).wait_recv()
        if orders[a] == "yx":
            second, third = outs[a].at[f, :, 1 - y, other], outs[a].at[1 - f, :, :, other]
        else:
            second, third = outs[a].at[1 - f, :, y, other], outs[a].at[:, :, 1 - y, other]
        remote(second, second, a, groups + 2, core).wait_recv()
        remote(third, third, a, groups + 3, core).wait_recv()
    for copy in started:
        copy.wait_send()


def gather(shards, orders, identity):
    n_f, n_s = lax.axis_size("fsdp"), lax.axis_size("seq")
    groups = n_s // 4
    count = len(shards)
    results = pl.pallas_call(
        partial(gather_kernel, groups, tuple(orders)),
        out_shape=[
            jax.ShapeDtypeStruct((n_f, groups, 2, 2) + shard.shape, shard.dtype)
            for shard in shards
        ],
        in_specs=[pl.BlockSpec(memory_space=pltpu.VMEM)] * count,
        out_specs=[pl.BlockSpec(memory_space=pltpu.HBM)] * count,
        scratch_shapes=[
            pltpu.SemaphoreType.DMA((count, groups + 4)),
            pltpu.SemaphoreType.DMA((count, groups + 4)),
            pltpu.SemaphoreType.DMA((count,)),
        ],
        compiler_params=pltpu.CompilerParams(
            collective_id=identity, has_side_effects=True, vmem_limit_bytes=VMEM_LIMIT
        ),
        name=f"gather_{identity}",
    )(*shards)
    return [
        whole.reshape(n_f * n_s * shard.shape[0], shard.shape[1])
        for whole, shard in zip(results, shards)
    ]


def gather_seq_kernel(groups, count, *refs):
    ins, outs = refs[:count], refs[count : 2 * count]
    send, recv, local = refs[2 * count :]
    f, z, y, c = place(groups)
    greet(groups, False)

    def remote(src, dst, a, slot, peer):
        return pltpu.make_async_remote_copy(
            src_ref=src,
            dst_ref=dst,
            send_sem=send.at[a, slot],
            recv_sem=recv.at[a, slot],
            device_id=peer,
            device_id_type=MESH,
        )

    core = device(f, z, y, 1 - c)
    side = device(f, z, 1 - y, c)
    started = []

    def start(copy):
        copy.start()
        started.append(copy)

    for a in range(count):
        pltpu.make_async_copy(ins[a], outs[a].at[z, y, c], local.at[a]).start()
        for d in range(1, groups):
            start(
                remote(
                    ins[a], outs[a].at[z, y, c], a, d, device(f, lax.rem(z + d, groups), y, c)
                )
            )
    for a in range(count):
        pltpu.make_async_copy(ins[a], outs[a].at[z, y, c], local.at[a]).wait()
        for d in range(1, groups):
            block = outs[a].at[lax.rem(z + groups - d, groups), y, c]
            remote(block, block, a, d, core).wait_recv()
        mine = outs[a].at[:, y, c]
        start(remote(mine, mine, a, 0, side))
        start(remote(mine, mine, a, groups, core))
    for a in range(count):
        got = outs[a].at[:, 1 - y, c]
        remote(got, got, a, 0, core).wait_recv()
        start(remote(got, got, a, groups + 1, core))
    for a in range(count):
        block = outs[a].at[:, y, 1 - c]
        remote(block, block, a, groups, core).wait_recv()
        block = outs[a].at[:, 1 - y, 1 - c]
        remote(block, block, a, groups + 1, core).wait_recv()
    for copy in started:
        copy.wait_send()


def gather_seq(shards, identity):
    n_s = lax.axis_size("seq")
    groups = n_s // 4
    count = len(shards)
    results = pl.pallas_call(
        partial(gather_seq_kernel, groups, count),
        out_shape=[
            jax.ShapeDtypeStruct((groups, 2, 2) + shard.shape, shard.dtype) for shard in shards
        ],
        in_specs=[pl.BlockSpec(memory_space=pltpu.VMEM)] * count,
        out_specs=[pl.BlockSpec(memory_space=pltpu.HBM)] * count,
        scratch_shapes=[
            pltpu.SemaphoreType.DMA((count, groups + 2)),
            pltpu.SemaphoreType.DMA((count, groups + 2)),
            pltpu.SemaphoreType.DMA((count,)),
        ],
        compiler_params=pltpu.CompilerParams(
            collective_id=identity, has_side_effects=True, vmem_limit_bytes=VMEM_LIMIT
        ),
        name=f"gather_seq_{identity}",
    )(*shards)
    return [
        whole.reshape(n_s * shard.shape[0], shard.shape[1])
        for whole, shard in zip(results, shards)
    ]


def scatter_kernel(groups, orders, *refs):
    count = len(orders)
    ins, outs = refs[:count], refs[count : 2 * count]
    held = refs[2 * count : 3 * count]
    from_core = refs[3 * count : 4 * count]
    from_first = refs[4 * count : 5 * count]
    from_second = refs[5 * count : 6 * count]
    from_z = refs[6 * count : 7 * count]
    send, recv, local = refs[7 * count :]
    f, z, y, c = place(groups)
    greet(groups, True)

    def remote(src, dst, a, slot, peer):
        return pltpu.make_async_remote_copy(
            src_ref=src,
            dst_ref=dst,
            send_sem=send.at[a, slot],
            recv_sem=recv.at[a, slot],
            device_id=peer,
            device_id_type=MESH,
        )

    core = device(f, z, y, 1 - c)
    across = {"y": device(f, z, 1 - y, c), "x": device(1 - f, z, y, c)}
    started = []

    def start(copy):
        copy.start()
        started.append(copy)

    def add(into, other):
        into[...] = (into[...].astype(F32) + other[...].astype(F32)).astype(BF16)

    for a in range(count):
        start(remote(ins[a].at[:, :, :, 1 - c], from_core[a], a, 0, core))
        pltpu.make_async_copy(ins[a].at[:, :, :, c], held[a], local.at[a]).start()
    for a in range(count):
        pltpu.make_async_copy(ins[a].at[:, :, :, c], held[a], local.at[a]).wait()
        remote(from_core[a], from_core[a], a, 0, core).wait_recv()
        if orders[a] == "xy":

            def part(g, carry, a=a):
                for k in range(2):
                    add(held[a].at[1 - f, g, k], from_core[a].at[1 - f, g, k])
                return carry

            lax.fori_loop(0, groups, part, 0)
            start(remote(held[a].at[1 - f], from_first[a], a, 1, across["x"]))

            def part(g, carry, a=a):
                for k in range(2):
                    add(held[a].at[f, g, k], from_core[a].at[f, g, k])
                return carry

            lax.fori_loop(0, groups, part, 0)
        else:

            def part(g, carry, a=a):
                for k in range(2):
                    add(held[a].at[k, g, 1 - y], from_core[a].at[k, g, 1 - y])
                return carry

            lax.fori_loop(0, groups, part, 0)
            start(remote(held[a].at[:, :, 1 - y], from_first[a], a, 1, across["y"]))

            def part(g, carry, a=a):
                for k in range(2):
                    add(held[a].at[k, g, y], from_core[a].at[k, g, y])
                return carry

            lax.fori_loop(0, groups, part, 0)
    for a in range(count):
        remote(from_first[a], from_first[a], a, 1, core).wait_recv()
        if orders[a] == "xy":

            def part(g, carry, a=a):
                for k in range(2):
                    add(held[a].at[f, g, k], from_first[a].at[g, k])
                return carry

            lax.fori_loop(0, groups, part, 0)
            start(remote(held[a].at[f, :, 1 - y], from_second[a], a, 2, across["y"]))
        else:

            def part(g, carry, a=a):
                for k in range(2):
                    add(held[a].at[k, g, y], from_first[a].at[k, g])
                return carry

            lax.fori_loop(0, groups, part, 0)
            start(remote(held[a].at[1 - f, :, y], from_second[a], a, 2, across["x"]))
    for a in range(count):
        remote(from_second[a], from_second[a], a, 2, core).wait_recv()

        def part(g, carry, a=a):
            add(held[a].at[f, g, y], from_second[a].at[g])
            return carry

        lax.fori_loop(0, groups, part, 0)
        for d in range(1, groups):
            there = lax.rem(z + d, groups)
            start(
                remote(held[a].at[f, there, y], from_z[a].at[d - 1], a, 2 + d, device(f, there, y, c))
            )
    for a in range(count):
        total = held[a][f, z, y].astype(F32)
        for d in range(1, groups):
            remote(from_z[a].at[d - 1], from_z[a].at[d - 1], a, 2 + d, core).wait_recv()
            total = total + from_z[a][d - 1].astype(F32)
        outs[a][...] = total
    for copy in started:
        copy.wait_send()


def scatter(partials, orders, identity):
    n_f, n_s = lax.axis_size("fsdp"), lax.axis_size("seq")
    groups = n_s // 4
    count = len(partials)
    blocks = [(p.shape[0] // (n_f * n_s), p.shape[1]) for p in partials]
    results = pl.pallas_call(
        partial(scatter_kernel, groups, tuple(orders)),
        out_shape=[jax.ShapeDtypeStruct(b, F32) for b in blocks],
        in_specs=[pl.BlockSpec(memory_space=pltpu.HBM)] * count,
        out_specs=[pl.BlockSpec(memory_space=pltpu.VMEM)] * count,
        scratch_shapes=[pltpu.VMEM((n_f, groups, 2) + b, BF16) for b in blocks]
        + [pltpu.VMEM((n_f, groups, 2) + b, BF16) for b in blocks]
        + [
            pltpu.VMEM(((groups, 2) if order == "xy" else (n_f, groups)) + b, BF16)
            for b, order in zip(blocks, orders)
        ]
        + [pltpu.VMEM((groups,) + b, BF16) for b in blocks]
        + [pltpu.VMEM((groups - 1,) + b, BF16) for b in blocks]
        + [
            pltpu.SemaphoreType.DMA((count, groups + 2)),
            pltpu.SemaphoreType.DMA((count, groups + 2)),
            pltpu.SemaphoreType.DMA((count,)),
        ],
        compiler_params=pltpu.CompilerParams(
            collective_id=identity, has_side_effects=True, vmem_limit_bytes=VMEM_LIMIT
        ),
        name=f"scatter_{identity}",
    )(*[p.reshape((n_f, groups, 2, 2) + b) for p, b in zip(partials, blocks)])
    return results


def scatter_seq_kernel(groups, in_ref, out_ref, held, from_core, from_y, from_z, send, recv, local):
    f, z, y, c = place(groups)
    greet(groups, False)

    def remote(src, dst, slot, peer):
        return pltpu.make_async_remote_copy(
            src_ref=src,
            dst_ref=dst,
            send_sem=send.at[slot],
            recv_sem=recv.at[slot],
            device_id=peer,
            device_id_type=MESH,
        )

    core = device(f, z, y, 1 - c)
    side = device(f, z, 1 - y, c)
    started = []

    def start(copy):
        copy.start()
        started.append(copy)

    def add(into, other):
        into[...] = (into[...].astype(F32) + other[...].astype(F32)).astype(BF16)

    start(remote(in_ref.at[:, :, 1 - c], from_core, 0, core))
    pltpu.make_async_copy(in_ref.at[:, :, c], held, local.at[0]).start()
    pltpu.make_async_copy(in_ref.at[:, :, c], held, local.at[0]).wait()
    remote(from_core, from_core, 0, core).wait_recv()

    def part(g, carry):
        add(held.at[g, 1 - y], from_core.at[g, 1 - y])
        return carry

    lax.fori_loop(0, groups, part, 0)
    start(remote(held.at[:, 1 - y], from_y, 1, side))

    def part(g, carry):
        add(held.at[g, y], from_core.at[g, y])
        return carry

    lax.fori_loop(0, groups, part, 0)
    remote(from_y, from_y, 1, side).wait_recv()

    def part(g, carry):
        add(held.at[g, y], from_y.at[g])
        return carry

    lax.fori_loop(0, groups, part, 0)
    for d in range(1, groups):
        there = lax.rem(z + d, groups)
        start(remote(held.at[there, y], from_z.at[d - 1], 1 + d, device(f, there, y, c)))
    total = held[z, y].astype(F32)
    for d in range(1, groups):
        remote(from_z.at[d - 1], from_z.at[d - 1], 1 + d, core).wait_recv()
        total = total + from_z[d - 1].astype(F32)
    out_ref[...] = total
    for copy in started:
        copy.wait_send()


def scatter_seq(partial_sums, identity):
    n_s = lax.axis_size("seq")
    groups = n_s // 4
    block = (partial_sums.shape[0] // n_s, partial_sums.shape[1])
    return pl.pallas_call(
        partial(scatter_seq_kernel, groups),
        out_shape=jax.ShapeDtypeStruct(block, F32),
        in_specs=[pl.BlockSpec(memory_space=pltpu.HBM)],
        out_specs=pl.BlockSpec(memory_space=pltpu.VMEM),
        scratch_shapes=[
            pltpu.VMEM((groups, 2) + block, BF16),
            pltpu.VMEM((groups, 2) + block, BF16),
            pltpu.VMEM((groups,) + block, BF16),
            pltpu.VMEM((groups - 1,) + block, BF16),
            pltpu.SemaphoreType.DMA((groups + 1,)),
            pltpu.SemaphoreType.DMA((groups + 1,)),
            pltpu.SemaphoreType.DMA((1,)),
        ],
        compiler_params=pltpu.CompilerParams(
            collective_id=identity, has_side_effects=True, vmem_limit_bytes=VMEM_LIMIT
        ),
        name=f"scatter_seq_{identity}",
    )(partial_sums.reshape((groups, 2, 2) + block))


def forward_kernel(span, bounds, query_ref, key_ref, value_ref, out_ref, norm_ref, stacked, peak, total):
    tokens = query_ref.shape[0]
    rows = tokens * HEADS
    scale = HEAD_DIM ** (-0.5)
    start, valid = bounds[0], bounds[1]
    for h in range(HEADS):
        stacked[h * tokens : (h + 1) * tokens, :] = query_ref[:, h * HEAD_DIM : (h + 1) * HEAD_DIM]
    peak[...] = jnp.full(peak.shape, -jnp.inf, F32)
    total[...] = jnp.zeros(total.shape, F32)
    out_ref[...] = jnp.zeros(out_ref.shape, F32)

    def block(j, masked):
        at = pl.multiple_of(j * span, span)
        keys = key_ref[pl.ds(at, span), :]
        values = value_ref[pl.ds(at, span), :]
        raw = times_transposed(stacked[...], keys) * scale
        if masked:
            key_pos = at + lax.broadcasted_iota(jnp.int32, (tokens, span), 1)
            row_pos = start + lax.broadcasted_iota(jnp.int32, (tokens, span), 0)
            allowed = (key_pos <= row_pos) & (key_pos < valid)
            raw = jnp.where(allowed[None], raw.reshape(HEADS, tokens, span), -jnp.inf)
            raw = raw.reshape(rows, span)
        old = peak[...]
        new = jnp.maximum(old, jnp.max(raw, axis=1, keepdims=True))
        shrink = jnp.exp(old - new)
        weights = jnp.exp(raw - new)
        total[...] = total[...] * shrink + jnp.sum(weights, axis=1, keepdims=True)
        out_ref[...] = out_ref[...] * shrink + matmul(weights.astype(BF16), values)
        peak[...] = new

    plain = jnp.minimum(start, valid) // span
    last = jnp.minimum(start + tokens, valid)
    every = (last + span - 1) // span

    def free(j, carry):
        block(j, False)
        return carry

    def edge(j, carry):
        block(j, True)
        return carry

    lax.fori_loop(0, plain, free, 0)
    lax.fori_loop(plain, every, edge, 0)
    out_ref[...] = out_ref[...] / total[...]
    norm_ref[...] = peak[...] + jnp.log(total[...])


def attention_forward(bounds, query, keys, values, span):
    tokens = query.shape[0]
    rows = tokens * HEADS
    return pl.pallas_call(
        partial(forward_kernel, span),
        out_shape=[
            jax.ShapeDtypeStruct((rows, HEAD_DIM), F32),
            jax.ShapeDtypeStruct((rows, 1), F32),
        ],
        in_specs=[pl.BlockSpec(memory_space=pltpu.SMEM)]
        + [pl.BlockSpec(memory_space=pltpu.VMEM)] * 3,
        out_specs=[pl.BlockSpec(memory_space=pltpu.VMEM)] * 2,
        scratch_shapes=[
            pltpu.VMEM((rows, HEAD_DIM), BF16),
            pltpu.VMEM((rows, 1), F32),
            pltpu.VMEM((rows, 1), F32),
        ],
        compiler_params=pltpu.CompilerParams(vmem_limit_bytes=VMEM_LIMIT),
        name="attention_forward",
    )(bounds, query, keys, values)


def backward_kernel(
    span, bounds, query_ref, grad_ref, key_ref, value_ref, norm_ref, delta_ref, gq_ref, gkv_ref, stacked, grads
):
    tokens = query_ref.shape[0]
    rows = tokens * HEADS
    scale = HEAD_DIM ** (-0.5)
    start, valid = bounds[0], bounds[1]
    for h in range(HEADS):
        columns = slice(h * HEAD_DIM, (h + 1) * HEAD_DIM)
        stacked[h * tokens : (h + 1) * tokens, :] = query_ref[:, columns]
        grads[h * tokens : (h + 1) * tokens, :] = grad_ref[:, columns]
    gq_ref[...] = jnp.zeros(gq_ref.shape, F32)

    def block(j, masked):
        at = pl.multiple_of(j * span, span)
        keys = key_ref[pl.ds(at, span), :]
        values = value_ref[pl.ds(at, span), :]
        raw = times_transposed(keys, stacked[...]) * scale
        soft = jnp.exp(raw - norm_ref[...])
        if masked:
            key_pos = at + lax.broadcasted_iota(jnp.int32, (span, tokens), 0)
            row_pos = start + lax.broadcasted_iota(jnp.int32, (span, tokens), 1)
            allowed = (key_pos <= row_pos) & (key_pos < valid)
            soft = jnp.where(jnp.concatenate([allowed] * HEADS, axis=1), soft, 0.0)
        toward = times_transposed(values, grads[...])
        pulled = (soft * (toward - delta_ref[...])).astype(BF16)
        gkv_ref[pl.ds(at, span), HEAD_DIM:] = matmul(soft.astype(BF16), grads[...]).astype(BF16)
        gkv_ref[pl.ds(at, span), :HEAD_DIM] = (matmul(pulled, stacked[...]) * scale).astype(BF16)
        gq_ref[...] += transposed_times(pulled, keys)

    plain = jnp.minimum(start, valid) // span
    last = jnp.minimum(start + tokens, valid)
    every = jnp.where(start < valid, (last + span - 1) // span, 0)
    plain = jnp.minimum(plain, every)

    def free(j, carry):
        block(j, False)
        return carry

    def edge(j, carry):
        block(j, True)
        return carry

    def empty(j, carry):
        at = pl.multiple_of(j * span, span)
        gkv_ref[pl.ds(at, span), :] = jnp.zeros((span, 2 * HEAD_DIM), BF16)
        return carry

    lax.fori_loop(0, plain, free, 0)
    lax.fori_loop(plain, every, edge, 0)
    lax.fori_loop(every, key_ref.shape[0] // span, empty, 0)
    gq_ref[...] = gq_ref[...] * scale


def attention_backward(bounds, query, grad, keys, values, norm, delta, span):
    tokens = query.shape[0]
    rows = tokens * HEADS
    return pl.pallas_call(
        partial(backward_kernel, span),
        out_shape=[
            jax.ShapeDtypeStruct((rows, HEAD_DIM), F32),
            jax.ShapeDtypeStruct((keys.shape[0], 2 * HEAD_DIM), BF16),
        ],
        in_specs=[pl.BlockSpec(memory_space=pltpu.SMEM)]
        + [pl.BlockSpec(memory_space=pltpu.VMEM)] * 6,
        out_specs=[pl.BlockSpec(memory_space=pltpu.VMEM)] * 2,
        scratch_shapes=[
            pltpu.VMEM((rows, HEAD_DIM), BF16),
            pltpu.VMEM((rows, HEAD_DIM), BF16),
        ],
        compiler_params=pltpu.CompilerParams(vmem_limit_bytes=VMEM_LIMIT),
        name="attention_backward",
    )(bounds, query, grad, keys, values, norm, delta)


def heads_to_columns(stacked):
    tokens = stacked.shape[0] // HEADS
    return jnp.concatenate([stacked[h * tokens : (h + 1) * tokens] for h in range(HEADS)], axis=1)


def gain_shard(gain):
    return jnp.zeros((8, 128), BF16).at[0, : gain.shape[0]].set(gain)


def gain_whole(gathered, rows):
    return gathered.reshape(-1, 8, 128)[:, 0, :rows].reshape(-1).astype(F32)


def gain_partial(grad, rows):
    count = grad.shape[0] // rows
    return jnp.pad(
        grad.astype(BF16).reshape(count, 1, rows), ((0, 0), (0, 7), (0, 128 - rows))
    ).reshape(count * 8, 128)


def per_device(
    hidden_in,
    cotangent,
    dataset_ids,
    mixing,
    pad_lengths,
    attention_gain,
    merged_projection,
    merged_adapter_in,
    query_adapter_out,
    keyval_adapter_out,
    output_projection,
    output_adapter_in,
    output_adapter_out,
    feedforward_gain,
    gate_up_weight,
    gate_up_adapter_in,
    gate_up_adapter_out,
    down_weight,
    down_adapter_in,
    down_adapter_out,
):
    tokens = hidden_in.shape[0]
    query_width = HEADS * HEAD_DIM
    model_rows = merged_projection.shape[0]
    rank_rows = query_adapter_out.shape[0]
    pair_rows = keyval_adapter_out.shape[0]
    out_rows = output_projection.shape[0]
    ff_rows = down_weight.shape[0]

    gain_one, merged, adapt_merged, lift_query, lift_keyval = gather(
        [
            gain_shard(attention_gain),
            pad_shard(merged_projection),
            pad_shard(merged_adapter_in),
            pad_shard(query_adapter_out),
            pad_shard(keyval_adapter_out),
        ],
        ["xy", "yx", "xy", "xy", "xy"],
        0,
    )
    out_full, adapt_out, lift_out, gain_two, gate_up, adapt_gate_up, lift_gate_up, down, adapt_down, lift_down = gather(
        [
            pad_shard(output_projection),
            pad_shard(output_adapter_in),
            pad_shard(output_adapter_out),
            gain_shard(feedforward_gain),
            pad_shard(gate_up_weight),
            pad_shard(gate_up_adapter_in),
            pad_shard(gate_up_adapter_out),
            pad_shard(down_weight),
            pad_shard(down_adapter_in),
            pad_shard(down_adapter_out),
        ],
        ["yx", "xy", "xy", "xy", "yx", "xy", "xy", "xy", "xy", "xy"],
        1,
    )
    gain_one = gain_whole(gain_one, model_rows)
    gain_two = gain_whole(gain_two, model_rows)

    hidden = hidden_in.astype(F32)
    normed_one, norm_one_back = jax.vjp(rms_scale, hidden, gain_one)
    first_in = spread(normed_one.astype(BF16), model_rows)
    projected = matmul(first_in, merged)
    lifted = matmul(first_in, adapt_merged).astype(BF16)
    lifted_query = spread(lifted[:, :RANK], rank_rows)
    lifted_pair = spread(lifted[:, RANK:], pair_rows)
    half_pair = lifted_pair.shape[1] // 2
    query_rows = projected[:, :query_width] + matmul(lifted_query, lift_query)
    key_rows = projected[:, query_width : query_width + HEAD_DIM] + matmul(
        lifted_pair[:, :half_pair], lift_keyval[:half_pair]
    )
    value_rows = projected[:, query_width + HEAD_DIM :] + matmul(
        lifted_pair[:, half_pair:], lift_keyval[half_pair:]
    )
    start_pos = lax.axis_index("seq") * tokens
    positions = start_pos + jnp.arange(tokens, dtype=jnp.int32)
    cosine_table, sine_table = rotary_tables(positions)
    query_rot = rotate_heads(query_rows, cosine_table, sine_table).astype(BF16)
    keys_rot = rotate(key_rows, cosine_table, sine_table).astype(BF16)
    keys_all, values_all = gather_seq([keys_rot, value_rows.astype(BF16)], 2)
    length = keys_all.shape[0]
    valid_count = length - pad_lengths[0]
    span = min(512, length)
    bounds = jnp.stack([start_pos, valid_count])

    attended, log_norm = attention_forward(bounds, query_rot, keys_all, values_all, span)
    attended_low = heads_to_columns(attended.astype(BF16))
    out_base = matmul(attended_low, out_full)
    lifted_out = matmul(attended_low, adapt_out).astype(BF16)
    lifted_out_wide = spread(lifted_out, rank_rows)
    middle = hidden + (out_base + matmul(lifted_out_wide, lift_out))

    normed_two, norm_two_back = jax.vjp(rms_scale, middle, gain_two)
    second_in = spread(normed_two.astype(BF16), model_rows)
    pre_gate = matmul(second_in, gate_up)
    lifted_gate_up = spread(matmul(second_in, adapt_gate_up).astype(BF16), pair_rows)
    half_gate = lifted_gate_up.shape[1] // 2
    gate_part = pre_gate[:, :FF] + matmul(lifted_gate_up[:, :half_gate], lift_gate_up[:half_gate])
    upper_part = pre_gate[:, FF:] + matmul(lifted_gate_up[:, half_gate:], lift_gate_up[half_gate:])
    activated, gelu_back = jax.vjp(partial(jax.nn.gelu, approximate=True), gate_part)
    inner = spread((activated * upper_part).astype(BF16), ff_rows)
    down_base = matmul(inner, down)
    lifted_down = spread(matmul(inner, adapt_down).astype(BF16), rank_rows)
    output = middle + (down_base + matmul(lifted_down, lift_down))

    matches = dataset_ids[:, None] == jnp.arange(DATASETS, dtype=jnp.int32)[None, :]
    picked = jnp.sum(jnp.where(matches, mixing[None, :], 0.0), axis=1)
    row_weight = jnp.where(positions < valid_count, picked, 0.0)
    scaled = cotangent.astype(F32) * row_weight[:, None]

    grad_branch = scaled.astype(BF16)
    grad_lifted_down = collect(times_transposed(grad_branch, lift_down), rank_rows).astype(BF16)
    grad_inner = collect(
        times_transposed(grad_branch, down) + times_transposed(grad_lifted_down, adapt_down), ff_rows
    )
    grad_gate = gelu_back(grad_inner * upper_part)[0].astype(BF16)
    grad_upper = (grad_inner * activated).astype(BF16)
    grad_gate_up = jnp.concatenate([grad_gate, grad_upper], axis=1)
    grad_lifted_gate_up = jnp.concatenate(
        [
            collect(times_transposed(grad_gate, lift_gate_up[:half_gate]), pair_rows),
            collect(times_transposed(grad_upper, lift_gate_up[half_gate:]), pair_rows),
        ],
        axis=1,
    ).astype(BF16)
    grad_normed_two = collect(
        times_transposed(grad_gate_up, gate_up)
        + times_transposed(grad_lifted_gate_up, adapt_gate_up),
        model_rows,
    )
    grad_middle_norm, gain_two_grad = norm_two_back(grad_normed_two)
    grad_middle = scaled + grad_middle_norm

    grad_attn = grad_middle.astype(BF16)
    grad_lifted_out = collect(times_transposed(grad_attn, lift_out), rank_rows).astype(BF16)
    grad_attention = (
        times_transposed(grad_attn, out_full) + times_transposed(grad_lifted_out, adapt_out)
    ).astype(BF16)
    correction = jnp.concatenate(
        [
            jnp.sum(
                grad_attention[:, h * HEAD_DIM : (h + 1) * HEAD_DIM].astype(F32)
                * attended[h * tokens : (h + 1) * tokens],
                axis=1,
            )
            for h in range(HEADS)
        ]
    )
    grad_query_rot, kv_terms = attention_backward(
        bounds,
        query_rot,
        grad_attention,
        keys_all,
        values_all,
        log_norm.reshape(1, -1),
        correction.reshape(1, -1),
        span,
    )
    kv_summed = scatter_seq(kv_terms, 3)
    grad_query_pre = rotate_heads(heads_to_columns(grad_query_rot), cosine_table, -sine_table)
    grad_keys = rotate(kv_summed[:, :HEAD_DIM], cosine_table, -sine_table)
    grad_merged = jnp.concatenate(
        [grad_query_pre.astype(BF16), grad_keys.astype(BF16), kv_summed[:, HEAD_DIM:].astype(BF16)],
        axis=1,
    )
    grad_lifted = jnp.concatenate(
        [
            collect(times_transposed(grad_merged[:, :query_width], lift_query), rank_rows),
            collect(
                times_transposed(
                    grad_merged[:, query_width : query_width + HEAD_DIM], lift_keyval[:half_pair]
                ),
                pair_rows,
            ),
            collect(
                times_transposed(grad_merged[:, query_width + HEAD_DIM :], lift_keyval[half_pair:]),
                pair_rows,
            ),
        ],
        axis=1,
    ).astype(BF16)
    grad_normed_one = collect(
        times_transposed(grad_merged, merged) + times_transposed(grad_lifted, adapt_merged),
        model_rows,
    )
    grad_hidden_norm, gain_one_grad = norm_one_back(grad_normed_one)
    hidden_grad = grad_middle + grad_hidden_norm

    keyval_term = jnp.concatenate(
        [
            transposed_times(
                lifted_pair[:, :half_pair], grad_merged[:, query_width : query_width + HEAD_DIM], BF16
            ),
            transposed_times(
                lifted_pair[:, half_pair:], grad_merged[:, query_width + HEAD_DIM :], BF16
            ),
        ],
        axis=0,
    )
    gate_up_term = jnp.concatenate(
        [
            transposed_times(lifted_gate_up[:, :half_gate], grad_gate, BF16),
            transposed_times(lifted_gate_up[:, half_gate:], grad_upper, BF16),
        ],
        axis=0,
    )
    summed = scatter(
        [
            transposed_times(second_in, grad_gate_up, BF16),
            transposed_times(inner, grad_branch, BF16),
            gate_up_term,
            transposed_times(first_in, grad_merged, BF16),
            transposed_times(attended_low, grad_attn, BF16),
            transposed_times(first_in, grad_lifted, BF16),
            transposed_times(inner, grad_lifted_down, BF16),
            transposed_times(second_in, grad_lifted_gate_up, BF16),
            transposed_times(lifted_query, grad_merged[:, :query_width], BF16),
            transposed_times(attended_low, grad_lifted_out, BF16),
            transposed_times(lifted_out_wide, grad_attn, BF16),
            transposed_times(lifted_down, grad_branch, BF16),
            keyval_term,
            gain_partial(gain_one_grad, model_rows),
            gain_partial(gain_two_grad, model_rows),
        ],
        ["xy", "yx", "yx", "xy", "xy", "yx", "yx", "yx", "yx", "yx", "yx", "yx", "yx", "yx", "yx"],
        4,
    )
    (
        gate_up_sum,
        down_sum,
        gate_up_out_sum,
        merged_sum,
        out_proj_sum,
        merged_in_sum,
        down_in_sum,
        gate_up_in_sum,
        query_out_sum,
        out_in_sum,
        out_out_sum,
        down_out_sum,
        keyval_sum,
        gain_one_sum,
        gain_two_sum,
    ) = summed
    return (
        output.astype(BF16),
        hidden_grad.astype(BF16),
        gain_one_sum[0, :model_rows],
        merged_sum[:model_rows],
        merged_in_sum[:model_rows],
        query_out_sum[:rank_rows],
        keyval_sum[:pair_rows],
        out_proj_sum[:out_rows],
        out_in_sum[:out_rows],
        out_out_sum[:rank_rows],
        gain_two_sum[0, :model_rows],
        gate_up_sum[:model_rows],
        gate_up_in_sum[:model_rows],
        gate_up_out_sum[:pair_rows],
        down_sum[:ff_rows],
        down_in_sum[:ff_rows],
        down_out_sum[:rank_rows],
    )


def solution(mesh):
    rows, vector = P(AXES, None), P(AXES)
    return jax.shard_map(
        per_device,
        mesh=mesh,
        in_specs=(rows, rows, vector, P(), P("fsdp"), vector)
        + (rows,) * 7
        + (vector,)
        + (rows,) * 6,
        out_specs=(rows, rows, vector) + (rows,) * 7 + (vector,) + (rows,) * 6,
        check_vma=False,
    )
```

time: 1750 us -> 549 us (0.31)
  waiting for transfers between devices: 811 us -> 0 us
  blocking collectives: 606 us -> 0 us
  Pallas kernels: 0 us -> 419 us
  starting transfers between devices: 80.2 us -> 0 us
  local copies, waits for them, and re-layouts: 83.6 us -> 39.8 us
  loops' own time: 33 us -> 0 us
  matrix products: 86.2 us -> 55.9 us
    reduce_scatter x8 -> x0, waiting for transfers between devices: 701 us -> none  [the longest x1 144 us: weight_gradient(): lax.psum_scatter(transposed_times(lax.slice_in_dim(activations, 0, shard_...]
    pallas_call x0 -> x7, Pallas kernels: none -> 419 us  [the longest x2 163 us: gather(): pl.pallas_call(partial(gather_kernel, groups, tuple(orders)), out_shape=[...]
    unnamed x3 -> x0, blocking collectives: 322 us -> none
    all_gather x7 -> x0, blocking collectives: 285 us -> none  [the longest x1 44.5 us: per_device(): lax.all_gather(merged_adapter_in, ('fsdp', 'seq'), axis=0, tiled=True)]
    unnamed x25 -> x0, starting transfers between devices: 79.3 us -> none
    unnamed x42 -> x0, waiting for transfers between devices: 78.1 us -> none
    another operation x27 -> x0, loops' own time: 33 us -> none  [the longest x3 32.5 us: blockwise(): return lax.scan(guarded, initial, (block_starts, key_blocks, value_blocks))]
    all_gather x8 -> x0, waiting for transfers between devices: 32.1 us -> none  [the longest x1 32 us: per_device(): lax.all_gather(gate_up_adapter_out, ('fsdp', 'seq'), axis=0, tiled=True)]
  transfers between devices with their start and end apart: 41 -> 0, of which waited for: 9 -> 0; matrix products, arithmetic and copies ran while one was open for 23% -> 0% of each run, Pallas kernels for 0% -> 0%
where the time goes in v1:
time: 549 us; the launch traced here: 541 us
  Pallas kernels  419 us (76%)
  matrix products  55.9 us (10%)
  local copies, waits for them, and re-layouts  39.8 us (7%)
  other arithmetic  23 us (4%)
    pallas_call x2, Pallas kernels, gather(): pl.pallas_call(partial(gather_kernel, groups, tuple(orders)), out_shape=[...  163 us
    pallas_call x1, Pallas kernels, scatter(): pl.pallas_call(partial(scatter_kernel, groups, tuple(orders)), out_shape=...  140 us
    pallas_call x1, Pallas kernels, scatter_seq(): pl.pallas_call(partial(scatter_seq_kernel, groups), out_shape=jax.ShapeDt...  60.9 us
    pallas_call x1, Pallas kernels, gather_seq(): pl.pallas_call(partial(gather_seq_kernel, groups, count), out_shape=[jax....  41.3 us
    dot_general x15, matrix products, transposed_times(): lax.dot_general(left_side, right_side, (((0,), (0,)), ((), ())), preferre...  25.8 us
    unnamed x197, local copies, waits for them, and re-layouts  22.2 us
    dot_general x17, matrix products, matmul(): return jnp.dot(left_side, right_side, preferred_element_type=F32)  15.1 us
    dot_general x21, matrix products, times_transposed(): lax.dot_general(left_side, right_side, (((1,), (1,)), ((), ())), preferre...  15.1 us

profile of v1, /device:TPU:0, one launch (start us, length us, event | category | flops | bytes accessed | tf_op | source)
XLA Modules:
  0.0 540.8 jit_solution(6824815620956567624)
XLA Ops:
  1.9 1.1 fusion.21
  3.5 0.8 select_reduce_fusion
  4.3 1.2 scatter.6.refs_0_
  5.6 1.2 scatter.9.refs_3_
  6.9 1.4 pad.35.refs_5_
  8.2 1.4 pad.33.refs_2_
  9.6 1.5 pad.32.refs_1_
  11.2 1.6 pad.34.refs_4_
  12.8 39.5 %gather_0.1 = (bf16[2,4,2,2,8,128]{5,4,3,2,1,0:T(8,128)(2,1)}, bf16[2,4,2,2,24,1536]{5,4,3,2,1,0:T(8,128)(2,1)}, bf16[2,4,2,2,24,768]{5,4,3,2,1,0:T(8,128)(2,1)}...) custom-call(bf16[8,128]{1,0:T(8,128)(2,1)} %scatter.6.refs_0_, bf16[24,1536]{1,0:T(8,128)(2,1)} %pad.32.refs_1_, ...), custom_call_target="tpu_custom_call" | custom-call | tf_op jit(solution)/shard_map/gather_0/pallas_call | solution.py:214
  52.3 0.9 slice.307
  53.3 1.0 fusion.179
  54.3 1.8 convolution_convert_fusion.13
  56.7 0.8 fusion.180
  57.5 0.8 fusion.13.refs_1_
  64.9 41.3 %gather_seq_2.1 = (bf16[4,2,2,256,256]{4,3,2,1,0:T(8,128)(2,1)}, bf16[4,2,2,256,256]{4,3,2,1,0:T(8,128)(2,1)}) custom-call(bf16[256,256]{1,0:T(8,128)(2,1)} %pad_maximum_fusion.12.refs_0_, bf16[256,256]{1,0:T(8,128)(2,1)} %fusion.13.refs_1_), custom_call_target="tpu_custom_call" | custom-call | tf_op jit(solution)/shard_map/gather_seq_2/pallas_call | solution.py:295
  106.2 6.8 %attention_forward.1 = (f32[1024,256]{1,0:T(8,128)}, f32[1024,1]{1,0:T(8,128)}) custom-call(s32[2]{0:T(128)} %pad_add_fusion.bounds, bf16[256,1024]{1,0:T(8,128)(2,1)} %copy-done.19, bf16[4096,256]{1,0:T(8,128)(2,1)} %bitcast.123, bf16[4096,256]{1,0:T(8,128)(2,1)} %bitcast.125), custom_call_target="tpu_custom_call" | custom-call | tf_op jit(solution)/shard_map/attention_forward/pallas_call | solution.py:600
  113.0 1.8 reduce.4
  114.9 1.3 convert_element_type.236
  116.3 123.3 %gather_1.1 = (bf16[2,4,2,2,32,640]{5,4,3,2,1,0:T(8,128)(2,1)}, bf16[2,4,2,2,32,256]{5,4,3,2,1,0:T(8,128)(2,1)}, bf16[2,4,2,2,8,640]{5,4,3,2,1,0:T(8,128)(2,1)},...) custom-call(bf16[32,640]{1,0:T(8,128)(2,1)} %refs_0_.1, ...), custom_call_target="tpu_custom_call" | custom-call | tf_op jit(solution)/shard_map/gather_1/pallas_call | solution.py:214
  239.6 0.9 slice.328
  240.6 1.5 convolution_convert_fusion.20
  245.6 1.0 copy-done
  246.7 1.1 convolution_add_fusion
  249.3 1.9 fusion.182
  251.6 2.5 fusion.6
  255.1 1.8 fusion.9
  257.9 1.1 convolution_convert_fusion.14
  259.4 1.8 fusion.12
  261.1 1.3 convolution_convert_fusion.8
  263.8 1.3 multiply_reduce_fusion
  265.1 1.1 fusion.175
  268.9 7.3 %attention_backward.1 = (f32[1024,256]{1,0:T(8,128)}, bf16[4096,512]{1,0:T(8,128)(2,1)}) custom-call(s32[2]{0:T(128)} %pad_add_fusion.bounds, bf16[256,1024]{1,0:T(8,128)(2,1)} %copy-done.19, bf16[256,1024]{1,0:T(8,128)(2,1)} %copy-done.9, bf16[4096,256]{1,0:T(8,128)(2,1)} %bitcast.124, bf16[4096,256]{1,0:T(8,128)(2,1)} %bitcast.126, f32[1,1024]{1,0:T(1,128)} %bitcast.171, ...), custom_call_target="tpu_custom_call" | custom-call | tf_op jit(solution)/shard_map/attention_backward/pallas_call | solution.py:676
  276.2 60.9 %scatter_seq_3.1 = f32[256,512]{1,0:T(8,128)} custom-call(bf16[4,2,2,256,512]{4,3,2,1,0:T(8,128)(2,1)} %bitcast.136), custom_call_target="tpu_custom_call" | custom-call | tf_op jit(solution)/shard_map/scatter_seq_3/pallas_call | solution.py:528
  337.1 1.8 convolution_convert_fusion.23
  338.9 0.7 convert_element_type.291
  339.7 1.4 pad.37.clone
  341.1 1.2 convolution_convert_fusion.21
  342.4 2.1 convolution_convert_fusion.15
  344.5 2.3 convolution_convert_fusion.9
  346.8 1.7 convolution_convert_fusion.6
  353.8 1.1 convolution_convert_fusion.10
  356.9 0.8 fusion.186
  361.4 1.3 fusion.17
  362.7 0.9 fusion.20
  363.6 0.8 convert_element_type.290
  365.1 2.7 convolution_convert_fusion.7
  367.8 1.5 convolution_convert_fusion.3
  370.5 1.6 pad_maximum_fusion.1
  372.1 2.2 convolution_convert_fusion.1
  374.3 2.7 convolution_convert_fusion.2
  376.9 4.5 convolution_convert_fusion
  381.4 139.8 %scatter_4.1 = (f32[24,4096]{1,0:T(8,128)}, f32[64,640]{1,0:T(8,128)}, f32[16,2048]{1,0:T(8,128)}, f32[24,1536]{1,0:T(8,128)}, f32[32,640]{1,0:T(8,128)}, /*inde...) custom-call(bf16[2,4,2,2,24,4096]{5,4,3,2,1,0:T(8,128)(2,1)} %bitcas, ...), custom_call_target="tpu_custom_call" | custom-call | tf_op jit(solution)/shard_map/scatter_4/pallas_call | solution.py:437
  521.2 1.2 slice_bitcast_fusion.1
  522.5 1.2 slice_bitcast_fusion
  523.7 1.6 copy.93
  525.2 1.5 copy.94
  526.8 1.4 copy.95
  528.1 1.3 copy.96
  529.5 1.5 copy.97
  531.0 1.4 copy.98
  532.4 1.3 copy.99
  533.7 1.8 copy.100
  535.5 1.4 copy.101
  536.9 1.6 copy.102
  (257 shorter events, 34.4 us)
Async XLA Ops:
  3.5 52.6 %copy-start.65 = (f32[256]{0:T(256)}, f32[256]{0:T(256)S(1)}, u32[]{:S(2)}) copy-start(f32[256]{0:T(256)S(1)} %fusion.143) | copy-start | bytes 3076
  4.3 260.7 %copy-start.58 = (f32[256]{0:T(256)}, f32[256]{0:T(256)S(1)}, u32[]{:S(2)}) copy-start(f32[256]{0:T(256)S(1)} %compare_select_fusion) | copy-start | bytes 3076
  6.8 236.7 %copy-start.80 = (pred[768]{0:T(1024)(128)(4,1)}, pred[768]{0:T(1024)(128)(4,1)S(1)}, u32[]{:S(2)}) copy-start(pred[768]{0:T(1024)(128)(4,1)S(1)} %get-tuple-element.164) | copy-start | bytes 2308
  6.8 236.7 %copy-start.83 = (pred[768]{0:T(1024)(128)(4,1)}, pred[768]{0:T(1024)(128)(4,1)S(1)}, u32[]{:S(2)}) copy-start(pred[768]{0:T(1024)(128)(4,1)S(1)} %get-tuple-element.165) | copy-start | bytes 2308
  6.8 236.7 %copy-start.67 = (s32[768]{0:T(1024)}, s32[768]{0:T(1024)S(1)}, u32[]{:S(2)}) copy-start(s32[768]{0:T(1024)S(1)} %get-tuple-element.162) | copy-start | bytes 9220
  6.8 236.7 %copy-start.70 = (s32[768]{0:T(1024)}, s32[768]{0:T(1024)S(1)}, u32[]{:S(2)}) copy-start(s32[768]{0:T(1024)S(1)} %get-tuple-element.163) | copy-start | bytes 9220
  6.9 236.7 %copy-start.73 = (s32[768]{0:T(1024)}, s32[768]{0:T(1024)S(1)}, u32[]{:S(2)}) copy-start(s32[768]{0:T(1024)S(1)} %get-tuple-element.160) | copy-start | bytes 9220
  6.9 236.7 %copy-start.76 = (s32[768]{0:T(1024)}, s32[768]{0:T(1024)S(1)}, u32[]{:S(2)}) copy-start(s32[768]{0:T(1024)S(1)} %get-tuple-element.161) | copy-start | bytes 9220
  54.3 3.2 copy-start.34
  54.3 4.0 copy-start.32
  54.3 1.8 copy-start.7
  54.3 2.3 copy-start.20
  56.6 1.9 copy-start.16
  56.6 1.9 copy-start.23
  64.9 41.3 %copy-start.19 = (bf16[256,1024]{1,0:T(8,128)(2,1)}, bf16[256,1024]{1,0:T(8,128)(2,1)S(1)}, u32[]{:S(2)}) copy-start(bf16[256,1024]{1,0:T(8,128)(2,1)S(1)} %fusion.128.query_ref) | copy-start | bytes 1572868
  116.2 126.0 %copy-start.2 = (bf16[256,640]{1,0:T(8,128)(2,1)S(1)}, bf16[256,640]{1,0:T(8,128)(2,1)}, u32[]{:S(2)}) copy-start(bf16[256,640]{1,0:T(8,128)(2,1)} %param.25) | copy-start | bytes 983044
  116.2 126.5 %copy-start.49 = (bf16[256,256]{1,0:T(8,128)(2,1)}, bf16[256,256]{1,0:T(8,128)(2,1)S(1)}, u32[]{:S(2)}) copy-start(bf16[256,256]{1,0:T(8,128)(2,1)S(1)} %get-tuple-element.148) | copy-start | bytes 393220
  116.2 126.5 %copy-start.51 = (bf16[256,256]{1,0:T(8,128)(2,1)}, bf16[256,256]{1,0:T(8,128)(2,1)S(1)}, u32[]{:S(2)}) copy-start(bf16[256,256]{1,0:T(8,128)(2,1)S(1)} %get-tuple-element.149) | copy-start | bytes 393220
  116.2 126.5 %copy-start.53 = (bf16[256,256]{1,0:T(8,128)(2,1)}, bf16[256,256]{1,0:T(8,128)(2,1)S(1)}, u32[]{:S(2)}) copy-start(bf16[256,256]{1,0:T(8,128)(2,1)S(1)} %get-tuple-element.150) | copy-start | bytes 393220
  116.2 126.5 %copy-start.55 = (bf16[256,256]{1,0:T(8,128)(2,1)}, bf16[256,256]{1,0:T(8,128)(2,1)S(1)}, u32[]{:S(2)}) copy-start(bf16[256,256]{1,0:T(8,128)(2,1)S(1)} %get-tuple-element.151) | copy-start | bytes 393220
  239.6 2.6 copy-start.46
  239.6 2.9 copy-start.30
  240.6 3.0 copy-start.61
  240.6 2.2 copy-start.27
  240.6 2.2 copy-start.28
  242.5 2.6 copy-start.39
  244.7 1.9 copy-start
  245.1 6.5 %copy-start.25 = (bf16[256,512]{1,0:T(8,128)(2,1)}, bf16[256,512]{1,0:T(8,128)(2,1)S(1)}, u32[]{:S(2)}) copy-start(bf16[256,512]{1,0:T(8,128)(2,1)S(1)} %convolution_convert_fusion.16) | copy-start | bytes 786436
  245.1 3.5 slice-start
  246.7 1.8 copy-start.22
  246.7 2.6 slice-start.1
  257.4 1.6 copy-start.47
  259.3 3.1 copy-start.68
  259.3 3.1 copy-start.71
  259.3 3.1 copy-start.74
  259.4 3.1 copy-start.77
  259.4 3.1 copy-start.81
  259.4 3.1 copy-start.84
  265.1 1.7 copy-start.31
  276.2 60.9 %copy-start.35 = (bf16[1,4,2,2,16,256]{5,4,3,2,1,0:T(8,128)(2,1)S(1)}, bf16[1,4,2,2,16,256]{5,4,3,2,1,0:T(8,128)(2,1)}, u32[]{:S(2)}) copy-start(bf16[1,4,2,2,16,256]{5,4,3,2,1,0:T(8,128)(2,1)} %copy-done.34) | copy-start | bytes 393220
  276.2 62.7 %copy-start.79 = (bf16[640]{0:T(1024)(128)(2,1)S(1)}, bf16[640]{0:T(1024)(128)(2,1)}, u32[]{:S(2)}) copy-start(bf16[640]{0:T(1024)(128)(2,1)} %get-tuple-element.117) | copy-start | bytes 3844
  339.7 7.1 %copy-start.6 = (bf16[256,640]{1,0:T(8,128)(2,1)S(1)}, bf16[256,640]{1,0:T(8,128)(2,1)}, u32[]{:S(2)}) copy-start(bf16[256,640]{1,0:T(8,128)(2,1)} %copy-done.5) | copy-start | bytes 983044
  339.7 7.1 %copy-start.50 = (bf16[256,256]{1,0:T(8,128)(2,1)S(1)}, bf16[256,256]{1,0:T(8,128)(2,1)}, u32[]{:S(2)}) copy-start(bf16[256,256]{1,0:T(8,128)(2,1)} %copy-done.49) | copy-start | bytes 393220
  339.7 7.1 %copy-start.52 = (bf16[256,256]{1,0:T(8,128)(2,1)S(1)}, bf16[256,256]{1,0:T(8,128)(2,1)}, u32[]{:S(2)}) copy-start(bf16[256,256]{1,0:T(8,128)(2,1)} %copy-done.51) | copy-start | bytes 393220
  339.7 7.1 %copy-start.54 = (bf16[256,256]{1,0:T(8,128)(2,1)S(1)}, bf16[256,256]{1,0:T(8,128)(2,1)}, u32[]{:S(2)}) copy-start(bf16[256,256]{1,0:T(8,128)(2,1)} %copy-done.53) | copy-start | bytes 393220
  339.7 7.1 %copy-start.56 = (bf16[256,256]{1,0:T(8,128)(2,1)S(1)}, bf16[256,256]{1,0:T(8,128)(2,1)}, u32[]{:S(2)}) copy-start(bf16[256,256]{1,0:T(8,128)(2,1)} %copy-done.55) | copy-start | bytes 393220
  346.8 1.7 copy-start.10
  348.5 4.9 copy-start.24
  348.5 5.3 copy-start.17
  352.2 3.0 copy-start.1
  353.4 3.2 copy-start.33
  353.8 4.0 copy-start.41
  353.8 3.1 copy-start.21
  356.9 2.1 copy-start.36
  356.9 1.6 copy-start.8
  364.4 3.4 copy-start.40
  365.1 4.2 copy-start.26
  370.5 1.6 copy-start.14
  370.5 1.6 copy-start.37
  372.1 2.2 copy-start.4
  372.1 2.2 copy-start.59
  521.2 17.2 %copy-start.48 = (f32[64,640]{1,0:T(8,128)S(1)}, f32[64,640]{1,0:T(8,128)}, u32[]{:S(2)}) copy-start(f32[64,640]{1,0:T(8,128)} %get-tuple-element.197) | copy-start | bytes 491524
  521.2 17.9 %copy-start.57 = (f32[64,256]{1,0:T(8,128)S(1)}, f32[64,256]{1,0:T(8,128)}, u32[]{:S(2)}) copy-start(f32[64,256]{1,0:T(8,128)} %get-tuple-element.198) | copy-start | bytes 196612
  521.2 18.5 %copy-start.60 = (f32[8,640]{1,0:T(8,128)S(1)}, f32[8,640]{1,0:T(8,128)}, u32[]{:S(2)}) copy-start(f32[8,640]{1,0:T(8,128)} %get-tuple-element.199) | copy-start | bytes 61444
  (24 other events, 28.0 us)

commit v2 on v1

v2 whole, which is shorter than its diff:
```python
from functools import partial

import jax
import jax.numpy as jnp
from jax import lax
from jax.experimental import pallas as pl
from jax.experimental.pallas import tpu as pltpu
from jax.sharding import PartitionSpec as P

HEADS = 4
HEAD_DIM = 256
FF = 2048
RANK = 256
DATASETS = 16
EPSILON = 1e-06
MESH = pl.DeviceIdType.MESH
VMEM_LIMIT = 60 * 1024 * 1024
AXES = ("fsdp", "seq")
BF16 = jnp.bfloat16
F32 = jnp.float32


def rms_scale(values, gain_vector):
    inverse = lax.rsqrt(jnp.mean(values * values, axis=-1, keepdims=True) + EPSILON)
    return values * inverse * gain_vector


def rotary_tables(positions):
    half_width = HEAD_DIM // 2
    inverse = 10000.0 ** (-2.0 * jnp.arange(half_width, dtype=F32) / HEAD_DIM)
    angles = positions.astype(F32)[:, None] * inverse[None, :]
    return (jnp.cos(angles), jnp.sin(angles))


def rotate(values, cosine_table, sine_table):
    half_width = values.shape[-1] // 2
    first = values[..., :half_width]
    second = values[..., half_width:]
    return jnp.concatenate(
        [first * cosine_table - second * sine_table, second * cosine_table + first * sine_table],
        axis=-1,
    )


def rotate_heads(values, cosine_table, sine_table):
    parts = [
        rotate(values[:, h * HEAD_DIM : (h + 1) * HEAD_DIM], cosine_table, sine_table)
        for h in range(HEADS)
    ]
    return jnp.concatenate(parts, axis=1)


def matmul(left_side, right_side):
    return jnp.dot(left_side, right_side, preferred_element_type=F32)


def times_transposed(left_side, right_side):
    return lax.dot_general(
        left_side, right_side, (((1,), (1,)), ((), ())), preferred_element_type=F32
    )


def transposed_times(left_side, right_side, out=F32):
    return lax.dot_general(
        left_side, right_side, (((0,), (0,)), ((), ())), preferred_element_type=F32
    ).astype(out)


def padded_rows(rows):
    return -(-rows // 8) * 8


def padded_model_rows(rows):
    return -(-(rows + 1) // 8) * 8


def selection(rows, wide, count):
    source = lax.broadcasted_iota(jnp.int32, (count * rows, count * wide), 0)
    target = lax.broadcasted_iota(jnp.int32, (count * rows, count * wide), 1)
    inside = target % wide
    return ((source == target // wide * rows + inside) & (inside < rows)).astype(BF16)


def spread(values, rows, wide):
    if wide == rows:
        return values
    return matmul(values, selection(rows, wide, values.shape[1] // rows)).astype(BF16)


def collect(values, rows, wide):
    if wide == rows:
        return values
    chosen = selection(rows, wide, values.shape[1] // wide)
    first = values.astype(BF16)
    rest = values - first.astype(F32)
    second = rest.astype(BF16)
    third = (rest - second.astype(F32)).astype(BF16)
    return (
        times_transposed(first, chosen)
        + times_transposed(second, chosen)
        + times_transposed(third, chosen)
    )


def place(groups):
    f = lax.axis_index("fsdp")
    s = lax.axis_index("seq")
    c = lax.rem(s, 2)
    y = lax.rem(s // 2, 2)
    z = s // 4
    return f, z, y, c


def device(f, z, y, c):
    return (f, (z * 2 + y) * 2 + c)


def greet(groups, both):
    f, z, y, c = place(groups)
    barrier = pltpu.get_barrier_semaphore()
    peers = [device(f, z, y, 1 - c), device(f, z, 1 - y, c)]
    if both:
        peers.append(device(1 - f, z, y, c))
    for d in range(1, groups):
        peers.append(device(f, lax.rem(z + d, groups), y, c))
    for peer in peers:
        pl.semaphore_signal(barrier, inc=1, device_id=peer, device_id_type=MESH)
    pl.semaphore_wait(barrier, len(peers))


def pieces(rows, columns, target):
    count = max(1, min(columns // 128, round(rows * columns * 2 / target)))
    edges = [round(columns // 128 * i / count) * 128 for i in range(count)] + [columns]
    return [(lo, hi - lo) for lo, hi in zip(edges[:-1], edges[1:])]


def balanced(chunks, weight_first, loads):
    orders = []
    for bytes_each in chunks:
        light, heavy = (4, 8) if weight_first == "light" else (8, 4)
        xy = max(loads[0] + light * bytes_each, loads[1] + heavy * bytes_each)
        yx = max(loads[0] + heavy * bytes_each, loads[1] + light * bytes_each)
        if xy <= yx:
            orders.append("xy")
            loads = (loads[0] + light * bytes_each, loads[1] + heavy * bytes_each)
        else:
            orders.append("yx")
            loads = (loads[0] + heavy * bytes_each, loads[1] + light * bytes_each)
    return orders


def mixed(rows_jobs, jobs):
    step = MIX * len(jobs) / max(1, len(rows_jobs))
    keyed = [(i * step, 0, job) for i, job in enumerate(rows_jobs)]
    keyed += [(float(i), 1, job) for i, job in enumerate(jobs)]
    return [job for _, _, job in sorted(keyed, key=lambda entry: entry[:2])]


def run_jobs(jobs, spacing):
    depth = max(len(stages) for stages in jobs)
    for tick in range(len(jobs) + spacing * (depth - 1)):
        for stage in reversed(range(depth)):
            j = tick - spacing * stage
            if 0 <= j < len(jobs) and stage < len(jobs[j]):
                jobs[j][stage]()


class Mover:
    def __init__(self, groups, send, recv, local):
        self.groups = groups
        self.send, self.recv, self.local = send, recv, local
        self.f, self.z, self.y, self.c = place(groups)
        f, z, y, c = self.f, self.z, self.y, self.c
        self.core = device(f, z, y, 1 - c)
        self.across = {"y": device(f, z, 1 - y, c), "x": device(1 - f, z, y, c)}
        self.started = []

    def along_z(self, d):
        return device(self.f, lax.rem(self.z + d, self.groups), self.y, self.c)

    def remote(self, src, dst, job, slot, peer):
        return pltpu.make_async_remote_copy(
            src_ref=src,
            dst_ref=dst,
            send_sem=self.send.at[job, slot],
            recv_sem=self.recv.at[job, slot],
            device_id=peer,
            device_id_type=MESH,
        )

    def start(self, src, dst, job, slot, peer):
        copy = self.remote(src, dst, job, slot, peer)
        copy.start()
        self.started.append(copy)

    def arrived(self, ref, job, slot):
        self.remote(ref, ref, job, slot, self.core).wait_recv()

    def drain(self):
        for copy in self.started:
            copy.wait_send()


def gather_job(m, job, order, source, whole, lo, width):
    groups, f, z, y, c = m.groups, m.f, m.z, m.y, m.c
    columns = slice(lo, lo + width)
    own = source.at[:, columns]

    def at(*index):
        return whole.at[index + (slice(None), columns)]

    every = slice(None)

    def begin():
        pltpu.make_async_copy(own, at(f, z, y, c), m.local.at[job]).start()
        for d in range(1, groups):
            m.start(own, at(f, z, y, c), job, d, m.along_z(d))

    def first():
        pltpu.make_async_copy(own, at(f, z, y, c), m.local.at[job]).wait()
        for d in range(1, groups):
            m.arrived(at(f, lax.rem(z + groups - d, groups), y, c), job, d)
        mine = at(f, every, y, c)
        m.start(mine, mine, job, 0, m.across[order[0]])
        m.start(mine, mine, job, groups, m.core)

    def second():
        if order == "yx":
            got, mine = at(f, every, 1 - y, c), at(f, every, every, c)
        else:
            got, mine = at(1 - f, every, y, c), at(every, every, y, c)
        m.arrived(got, job, 0)
        m.start(mine, mine, job, groups + 1, m.across[order[1]])
        m.start(got, got, job, groups + 2, m.core)

    def third():
        got = at(1 - f, every, every, c) if order == "yx" else at(every, every, 1 - y, c)
        m.arrived(got, job, groups + 1)
        m.start(got, got, job, groups + 3, m.core)

    def last():
        other = 1 - c
        m.arrived(at(f, every, y, other), job, groups)
        if order == "yx":
            m.arrived(at(f, every, 1 - y, other), job, groups + 2)
            m.arrived(at(1 - f, every, every, other), job, groups + 3)
        else:
            m.arrived(at(1 - f, every, y, other), job, groups + 2)
            m.arrived(at(every, every, 1 - y, other), job, groups + 3)

    return [begin, first, second, third, last]


def gather_rows_job(m, job, source, whole, lo, width):
    groups, z, y, c = m.groups, m.z, m.y, m.c
    columns = slice(lo, lo + width)
    own = source.at[:, columns]
    every = slice(None)

    def at(*index):
        return whole.at[index + (slice(None), columns)]

    def begin():
        pltpu.make_async_copy(own, at(z, y, c), m.local.at[job]).start()
        for d in range(1, groups):
            m.start(own, at(z, y, c), job, d, m.along_z(d))

    def first():
        pltpu.make_async_copy(own, at(z, y, c), m.local.at[job]).wait()
        for d in range(1, groups):
            m.arrived(at(lax.rem(z + groups - d, groups), y, c), job, d)
        mine = at(every, y, c)
        m.start(mine, mine, job, 0, m.across["y"])
        m.start(mine, mine, job, groups, m.core)

    def second():
        got = at(every, 1 - y, c)
        m.arrived(got, job, 0)
        m.start(got, got, job, groups + 1, m.core)

    def last():
        m.arrived(at(every, y, 1 - c), job, groups)
        m.arrived(at(every, 1 - y, 1 - c), job, groups + 1)

    return [begin, first, second, last]


MIX = 0.6
GATHER_BYTES = 20 * 1024
ROWS_BYTES = 32 * 1024
GATHER_SPACING = 3
SCATTER_BYTES = 20 * 1024
SCATTER_SPACING = 4


def gather_kernel(groups, plan, rows_plan, *refs):
    rows_count = len({entry[0] for entry in rows_plan})
    count = rows_count + len({entry[0] for entry in plan})
    ins, outs = refs[:count], refs[count : 2 * count]
    send, recv, local = refs[2 * count :]
    greet(groups, True)
    m = Mover(groups, send, recv, local)
    jobs = []
    for a, lo, width in rows_plan:
        jobs.append(gather_rows_job(m, len(jobs), ins[a], outs[a], lo, width))
    for a, lo, width, order in plan:
        jobs.append(gather_job(m, len(jobs), order, ins[rows_count + a], outs[rows_count + a], lo, width))
    run_jobs(mixed(jobs[: len(rows_plan)], jobs[len(rows_plan) :]), GATHER_SPACING)
    m.drain()


def gather(token_rows, shards, identity):
    n_f, n_s = lax.axis_size("fsdp"), lax.axis_size("seq")
    groups = n_s // 4
    rows_plan = [
        (a, lo, width)
        for a, block in enumerate(token_rows)
        for lo, width in pieces(block.shape[0], block.shape[1], ROWS_BYTES)
    ]
    cuts = [
        (a, lo, width)
        for a, shard in enumerate(shards)
        for lo, width in pieces(shard.shape[0], shard.shape[1], GATHER_BYTES)
    ]
    sizes = [shards[a].shape[0] * width for a, _, width in cuts]
    held = sum(4 * block.shape[0] * block.shape[1] for block in token_rows)
    orders = balanced(sizes, "light", (0, held))
    plan = [cut + (order,) for cut, order in zip(cuts, orders)]
    operands = list(token_rows) + list(shards)
    jobs = len(rows_plan) + len(plan)
    results = pl.pallas_call(
        partial(gather_kernel, groups, tuple(plan), tuple(rows_plan)),
        out_shape=[
            jax.ShapeDtypeStruct((groups, 2, 2) + block.shape, block.dtype) for block in token_rows
        ]
        + [
            jax.ShapeDtypeStruct((n_f, groups, 2, 2) + shard.shape, shard.dtype)
            for shard in shards
        ],
        in_specs=[pl.BlockSpec(memory_space=pltpu.VMEM)] * len(operands),
        out_specs=[pl.BlockSpec(memory_space=pltpu.HBM)] * len(operands),
        scratch_shapes=[
            pltpu.SemaphoreType.DMA((jobs, groups + 4)),
            pltpu.SemaphoreType.DMA((jobs, groups + 4)),
            pltpu.SemaphoreType.DMA((jobs,)),
        ],
        compiler_params=pltpu.CompilerParams(
            collective_id=identity, has_side_effects=True, vmem_limit_bytes=VMEM_LIMIT
        ),
        name=f"gather_{identity}",
    )(*operands)
    return [whole.reshape(-1, block.shape[1]) for whole, block in zip(results, operands)]


def scatter_job(m, job, order, source, out, lo, width, buffers):
    groups, f, z, y, c = m.groups, m.f, m.z, m.y, m.c
    columns = slice(lo, lo + width)
    every = slice(None)
    held, from_core, from_first, from_second, from_z = buffers

    def half(core):
        return source.at[:, :, :, core, :, columns]

    def add(into, other):
        into[...] = into[...] + other[...]

    def each(step):
        def part(g, carry):
            step(g)
            return carry

        lax.fori_loop(0, groups, part, 0)

    def begin():
        m.start(half(1 - c), from_core, job, 0, m.core)
        pltpu.make_async_copy(half(c), held, m.local.at[job]).start()

    def first():
        pltpu.make_async_copy(half(c), held, m.local.at[job]).wait()
        m.arrived(from_core, job, 0)
        if order == "xy":
            def pair(side):
                def step(g):
                    for k in range(2):
                        add(held.at[side, g, k], from_core.at[side, g, k])
                return step

            each(pair(1 - f))
            m.start(held.at[1 - f], from_first, job, 1, m.across["x"])
            each(pair(f))
        else:
            def pair(side):
                def step(g):
                    for k in range(2):
                        add(held.at[k, g, side], from_core.at[k, g, side])
                return step

            each(pair(1 - y))
            m.start(held.at[:, :, 1 - y], from_first, job, 1, m.across["y"])
            each(pair(y))

    def second():
        m.arrived(from_first, job, 1)
        if order == "xy":
            def side(k):
                return lambda g: add(held.at[f, g, k], from_first.at[g, k])

            each(side(1 - y))
            m.start(held.at[f, :, 1 - y], from_second, job, 2, m.across["y"])
            each(side(y))
        else:
            def side(k):
                return lambda g: add(held.at[k, g, y], from_first.at[k, g])

            each(side(1 - f))
            m.start(held.at[1 - f, :, y], from_second, job, 2, m.across["x"])
            each(side(f))

    def third():
        m.arrived(from_second, job, 2)
        each(lambda g: add(held.at[f, g, y], from_second.at[g]))
        for d in range(1, groups):
            there = lax.rem(z + d, groups)
            m.start(held.at[f, there, y], from_z.at[d - 1], job, 2 + d, m.along_z(d))

    def last():
        total = held[f, z, y].astype(F32)
        for d in range(1, groups):
            m.arrived(from_z.at[d - 1], job, 2 + d)
            total = total + from_z[d - 1].astype(F32)
        out[:, columns] = total

    return [begin, first, second, third, last]


def scatter_rows_job(m, job, source, out, lo, width, buffers):
    groups, z, y, c = m.groups, m.z, m.y, m.c
    columns = slice(lo, lo + width)
    held, from_core, from_y, from_z = buffers

    def half(core):
        return source.at[:, :, core, :, columns]

    def add(into, other):
        into[...] = into[...] + other[...]

    def each(step):
        def part(g, carry):
            step(g)
            return carry

        lax.fori_loop(0, groups, part, 0)

    def begin():
        m.start(half(1 - c), from_core, job, 0, m.core)
        pltpu.make_async_copy(half(c), held, m.local.at[job]).start()

    def first():
        pltpu.make_async_copy(half(c), held, m.local.at[job]).wait()
        m.arrived(from_core, job, 0)
        each(lambda g: add(held.at[g, 1 - y], from_core.at[g, 1 - y]))
        m.start(held.at[:, 1 - y], from_y, job, 1, m.across["y"])
        each(lambda g: add(held.at[g, y], from_core.at[g, y]))

    def second():
        m.arrived(from_y, job, 1)
        each(lambda g: add(held.at[g, y], from_y.at[g]))
        for d in range(1, groups):
            there = lax.rem(z + d, groups)
            m.start(held.at[there, y], from_z.at[d - 1], job, 2 + d, m.along_z(d))

    def last():
        total = held[z, y].astype(F32)
        for d in range(1, groups):
            m.arrived(from_z.at[d - 1], job, 2 + d)
            total = total + from_z[d - 1].astype(F32)
        out[:, columns] = total

    return [begin, first, second, last]


def scatter_kernel(groups, plan, rows_plan, rows_count, count, *refs):
    ins, outs = refs[:count], refs[count : 2 * count]
    send, recv, local = refs[2 * count : 2 * count + 3]
    scratch = list(refs[2 * count + 3 :])
    greet(groups, True)
    m = Mover(groups, send, recv, local)
    jobs = []
    for a, lo, width in rows_plan:
        buffers, scratch = scratch[:4], scratch[4:]
        jobs.append(scatter_rows_job(m, len(jobs), ins[a], outs[a], lo, width, buffers))
    for a, lo, width, order in plan:
        buffers, scratch = scratch[:5], scratch[5:]
        jobs.append(
            scatter_job(m, len(jobs), order, ins[rows_count + a], outs[rows_count + a], lo, width, buffers)
        )
    run_jobs(mixed(jobs[: len(rows_plan)], jobs[len(rows_plan) :]), SCATTER_SPACING)
    m.drain()


def scatter(token_rows, partials, identity):
    n_f, n_s = lax.axis_size("fsdp"), lax.axis_size("seq")
    groups = n_s // 4
    row_blocks = [(p.shape[0] // n_s, p.shape[1]) for p in token_rows]
    blocks = [(p.shape[0] // (n_f * n_s), p.shape[1]) for p in partials]
    rows_plan = [
        (a, lo, width)
        for a, block in enumerate(row_blocks)
        for lo, width in pieces(block[0], block[1], ROWS_BYTES)
    ]
    cuts = [
        (a, lo, width)
        for a, block in enumerate(blocks)
        for lo, width in pieces(block[0], block[1], SCATTER_BYTES)
    ]
    sizes = [blocks[a][0] * width for a, _, width in cuts]
    held = sum(4 * rows * columns for rows, columns in row_blocks)
    orders = balanced(sizes, "heavy", (0, held))
    plan = [cut + (order,) for cut, order in zip(cuts, orders)]
    jobs = len(rows_plan) + len(plan)
    scratch = []
    for a, _, width in rows_plan:
        block = (row_blocks[a][0], width)
        scratch += [
            pltpu.VMEM((groups, 2) + block, BF16),
            pltpu.VMEM((groups, 2) + block, BF16),
            pltpu.VMEM((groups,) + block, BF16),
            pltpu.VMEM((groups - 1,) + block, BF16),
        ]
    for a, _, width, order in plan:
        block = (blocks[a][0], width)
        scratch += [
            pltpu.VMEM((n_f, groups, 2) + block, BF16),
            pltpu.VMEM((n_f, groups, 2) + block, BF16),
            pltpu.VMEM(((groups, 2) if order == "xy" else (n_f, groups)) + block, BF16),
            pltpu.VMEM((groups,) + block, BF16),
            pltpu.VMEM((groups - 1,) + block, BF16),
        ]
    count = len(row_blocks) + len(blocks)
    return pl.pallas_call(
        partial(scatter_kernel, groups, tuple(plan), tuple(rows_plan), len(row_blocks), count),
        out_shape=[jax.ShapeDtypeStruct(b, F32) for b in row_blocks + blocks],
        in_specs=[pl.BlockSpec(memory_space=pltpu.HBM)] * count,
        out_specs=[pl.BlockSpec(memory_space=pltpu.VMEM)] * count,
        scratch_shapes=[
            pltpu.SemaphoreType.DMA((jobs, groups + 2)),
            pltpu.SemaphoreType.DMA((jobs, groups + 2)),
            pltpu.SemaphoreType.DMA((jobs,)),
        ]
        + scratch,
        compiler_params=pltpu.CompilerParams(
            collective_id=identity, has_side_effects=True, vmem_limit_bytes=VMEM_LIMIT
        ),
        name=f"scatter_{identity}",
    )(
        *[p.reshape((groups, 2, 2) + b) for p, b in zip(token_rows, row_blocks)],
        *[p.reshape((n_f, groups, 2, 2) + b) for p, b in zip(partials, blocks)],
    )


def finish_kernel(cuts, count, *refs):
    total = len(cuts)
    ins, outs = refs[:count], refs[count : count + total]
    staged, sems = refs[count + total : count + 2 * total], refs[count + 2 * total]
    for i, (a, rows, lo, width) in enumerate(cuts):
        staged[i][...] = ins[a][0:rows, lo : lo + width]
    for i in range(total):
        pltpu.make_async_copy(staged[i], outs[i], sems.at[i]).start()
    for i in range(total):
        pltpu.make_async_copy(staged[i], outs[i], sems.at[i]).wait()


def finish(sums, cuts):
    shapes = [(rows, width) for _, rows, _, width in cuts]
    return pl.pallas_call(
        partial(finish_kernel, tuple(cuts), len(sums)),
        out_shape=[jax.ShapeDtypeStruct(shape, F32) for shape in shapes],
        in_specs=[pl.BlockSpec(memory_space=pltpu.VMEM)] * len(sums),
        out_specs=[pl.BlockSpec(memory_space=pltpu.HBM)] * len(cuts),
        scratch_shapes=[pltpu.VMEM(shape, F32) for shape in shapes]
        + [pltpu.SemaphoreType.DMA((len(cuts),))],
        compiler_params=pltpu.CompilerParams(vmem_limit_bytes=VMEM_LIMIT),
        name="finish",
    )(*sums)


def forward_kernel(span, bounds, query_ref, key_ref, value_ref, out_ref, norm_ref, stacked, peak, total):
    tokens = query_ref.shape[0]
    rows = tokens * HEADS
    scale = HEAD_DIM ** (-0.5)
    start, valid = bounds[0], bounds[1]
    for h in range(HEADS):
        stacked[h * tokens : (h + 1) * tokens, :] = query_ref[:, h * HEAD_DIM : (h + 1) * HEAD_DIM]
    peak[...] = jnp.full(peak.shape, -jnp.inf, F32)
    total[...] = jnp.zeros(total.shape, F32)
    out_ref[...] = jnp.zeros(out_ref.shape, F32)

    def block(j, masked):
        at = pl.multiple_of(j * span, span)
        keys = key_ref[pl.ds(at, span), :]
        values = value_ref[pl.ds(at, span), :]
        raw = times_transposed(stacked[...], keys) * scale
        if masked:
            key_pos = at + lax.broadcasted_iota(jnp.int32, (tokens, span), 1)
            row_pos = start + lax.broadcasted_iota(jnp.int32, (tokens, span), 0)
            allowed = (key_pos <= row_pos) & (key_pos < valid)
            raw = jnp.where(allowed[None], raw.reshape(HEADS, tokens, span), -jnp.inf)
            raw = raw.reshape(rows, span)
        old = peak[...]
        new = jnp.maximum(old, jnp.max(raw, axis=1, keepdims=True))
        shrink = jnp.exp(old - new)
        weights = jnp.exp(raw - new)
        total[...] = total[...] * shrink + jnp.sum(weights, axis=1, keepdims=True)
        out_ref[...] = out_ref[...] * shrink + matmul(weights.astype(BF16), values)
        peak[...] = new

    plain = jnp.minimum(start, valid) // span
    last = jnp.minimum(start + tokens, valid)
    every = (last + span - 1) // span

    def free(j, carry):
        block(j, False)
        return carry

    def edge(j, carry):
        block(j, True)
        return carry

    lax.fori_loop(0, plain, free, 0)
    lax.fori_loop(plain, every, edge, 0)
    out_ref[...] = out_ref[...] / total[...]
    norm_ref[...] = peak[...] + jnp.log(total[...])


def attention_forward(bounds, query, keys, values, span):
    tokens = query.shape[0]
    rows = tokens * HEADS
    return pl.pallas_call(
        partial(forward_kernel, span),
        out_shape=[
            jax.ShapeDtypeStruct((rows, HEAD_DIM), F32),
            jax.ShapeDtypeStruct((rows, 1), F32),
        ],
        in_specs=[pl.BlockSpec(memory_space=pltpu.SMEM)]
        + [pl.BlockSpec(memory_space=pltpu.VMEM)] * 3,
        out_specs=[pl.BlockSpec(memory_space=pltpu.VMEM)] * 2,
        scratch_shapes=[
            pltpu.VMEM((rows, HEAD_DIM), BF16),
            pltpu.VMEM((rows, 1), F32),
            pltpu.VMEM((rows, 1), F32),
        ],
        compiler_params=pltpu.CompilerParams(vmem_limit_bytes=VMEM_LIMIT),
        name="attention_forward",
    )(bounds, query, keys, values)


def backward_kernel(
    span, bounds, query_ref, grad_ref, key_ref, value_ref, norm_ref, delta_ref, gq_ref, gkv_ref, stacked, grads
):
    tokens = query_ref.shape[0]
    rows = tokens * HEADS
    scale = HEAD_DIM ** (-0.5)
    start, valid = bounds[0], bounds[1]
    for h in range(HEADS):
        columns = slice(h * HEAD_DIM, (h + 1) * HEAD_DIM)
        stacked[h * tokens : (h + 1) * tokens, :] = query_ref[:, columns]
        grads[h * tokens : (h + 1) * tokens, :] = grad_ref[:, columns]
    gq_ref[...] = jnp.zeros(gq_ref.shape, F32)

    def block(j, masked):
        at = pl.multiple_of(j * span, span)
        keys = key_ref[pl.ds(at, span), :]
        values = value_ref[pl.ds(at, span), :]
        raw = times_transposed(keys, stacked[...]) * scale
        soft = jnp.exp(raw - norm_ref[...])
        if masked:
            key_pos = at + lax.broadcasted_iota(jnp.int32, (span, tokens), 0)
            row_pos = start + lax.broadcasted_iota(jnp.int32, (span, tokens), 1)
            allowed = (key_pos <= row_pos) & (key_pos < valid)
            soft = jnp.where(jnp.concatenate([allowed] * HEADS, axis=1), soft, 0.0)
        toward = times_transposed(values, grads[...])
        pulled = (soft * (toward - delta_ref[...])).astype(BF16)
        gkv_ref[pl.ds(at, span), HEAD_DIM:] = matmul(soft.astype(BF16), grads[...]).astype(BF16)
        gkv_ref[pl.ds(at, span), :HEAD_DIM] = (matmul(pulled, stacked[...]) * scale).astype(BF16)
        gq_ref[...] += transposed_times(pulled, keys)

    plain = jnp.minimum(start, valid) // span
    last = jnp.minimum(start + tokens, valid)
    every = jnp.where(start < valid, (last + span - 1) // span, 0)
    plain = jnp.minimum(plain, every)

    def free(j, carry):
        block(j, False)
        return carry

    def edge(j, carry):
        block(j, True)
        return carry

    def empty(j, carry):
        at = pl.multiple_of(j * span, span)
        gkv_ref[pl.ds(at, span), :] = jnp.zeros((span, 2 * HEAD_DIM), BF16)
        return carry

    lax.fori_loop(0, plain, free, 0)
    lax.fori_loop(plain, every, edge, 0)
    lax.fori_loop(every, key_ref.shape[0] // span, empty, 0)
    gq_ref[...] = gq_ref[...] * scale


def attention_backward(bounds, query, grad, keys, values, norm, delta, span):
    tokens = query.shape[0]
    rows = tokens * HEADS
    return pl.pallas_call(
        partial(backward_kernel, span),
        out_shape=[
            jax.ShapeDtypeStruct((rows, HEAD_DIM), F32),
            jax.ShapeDtypeStruct((keys.shape[0], 2 * HEAD_DIM), BF16),
        ],
        in_specs=[pl.BlockSpec(memory_space=pltpu.SMEM)]
        + [pl.BlockSpec(memory_space=pltpu.VMEM)] * 6,
        out_specs=[pl.BlockSpec(memory_space=pltpu.VMEM)] * 2,
        scratch_shapes=[
            pltpu.VMEM((rows, HEAD_DIM), BF16),
            pltpu.VMEM((rows, HEAD_DIM), BF16),
        ],
        compiler_params=pltpu.CompilerParams(vmem_limit_bytes=VMEM_LIMIT),
        name="attention_backward",
    )(bounds, query, grad, keys, values, norm, delta)


def heads_to_columns(stacked):
    tokens = stacked.shape[0] // HEADS
    return jnp.concatenate([stacked[h * tokens : (h + 1) * tokens] for h in range(HEADS)], axis=1)


def model_shard(first, second, gain):
    rows = first.shape[0]
    wide = padded_model_rows(rows)
    block = jnp.concatenate([first, second], axis=1)
    spare = jnp.pad(gain[None], ((0, wide - rows - 1), (0, block.shape[1] - rows)))
    return jnp.concatenate([block, spare], axis=0)


def plain_shard(*weights):
    block = weights[0] if len(weights) == 1 else jnp.concatenate(weights, axis=1)
    rows = block.shape[0]
    return jnp.pad(block, ((0, padded_rows(rows) - rows), (0, 0)))


def gain_whole(gathered, rows):
    wide = padded_model_rows(rows)
    return gathered.reshape(-1, wide, gathered.shape[1])[:, rows, :rows].reshape(-1).astype(F32)


def with_gain(partial_sums, gain_grad, rows):
    wide = padded_model_rows(rows)
    blocks = partial_sums.reshape(-1, wide, partial_sums.shape[1])
    return blocks.at[:, rows, :rows].set(gain_grad.reshape(-1, rows).astype(BF16)).reshape(partial_sums.shape)


def per_device(
    hidden_in,
    cotangent,
    dataset_ids,
    mixing,
    pad_lengths,
    attention_gain,
    merged_projection,
    merged_adapter_in,
    query_adapter_out,
    keyval_adapter_out,
    output_projection,
    output_adapter_in,
    output_adapter_out,
    feedforward_gain,
    gate_up_weight,
    gate_up_adapter_in,
    gate_up_adapter_out,
    down_weight,
    down_adapter_in,
    down_adapter_out,
):
    tokens, width = hidden_in.shape
    query_width = HEADS * HEAD_DIM
    merged_width = query_width + 2 * HEAD_DIM
    model_rows = merged_projection.shape[0]
    rank_rows = query_adapter_out.shape[0]
    pair_rows = keyval_adapter_out.shape[0]
    out_rows = output_projection.shape[0]
    ff_rows = down_weight.shape[0]
    model_wide, rank_wide = padded_model_rows(model_rows), padded_rows(rank_rows)
    pair_wide, ff_wide = padded_rows(pair_rows), padded_rows(ff_rows)

    merged, lift_query, lift_keyval = gather(
        [],
        [
            model_shard(merged_projection, merged_adapter_in, attention_gain),
            plain_shard(query_adapter_out),
            plain_shard(keyval_adapter_out),
        ],
        0,
    )
    gain_one = gain_whole(merged, model_rows)

    hidden = hidden_in.astype(F32)
    normed_one, norm_one_back = jax.vjp(rms_scale, hidden, gain_one)
    first_in = spread(normed_one.astype(BF16), model_rows, model_wide)
    projected = matmul(first_in, merged)
    lifted = projected[:, merged_width:].astype(BF16)
    lifted_query = spread(lifted[:, :RANK], rank_rows, rank_wide)
    lifted_pair = spread(lifted[:, RANK:], pair_rows, pair_wide)
    half_pair = lifted_pair.shape[1] // 2
    query_rows = projected[:, :query_width] + matmul(lifted_query, lift_query)
    key_rows = projected[:, query_width : query_width + HEAD_DIM] + matmul(
        lifted_pair[:, :half_pair], lift_keyval[:half_pair]
    )
    value_rows = projected[:, query_width + HEAD_DIM : merged_width] + matmul(
        lifted_pair[:, half_pair:], lift_keyval[half_pair:]
    )
    start_pos = lax.axis_index("seq") * tokens
    positions = start_pos + jnp.arange(tokens, dtype=jnp.int32)
    cosine_table, sine_table = rotary_tables(positions)
    query_rot = rotate_heads(query_rows, cosine_table, sine_table).astype(BF16)
    keys_rot = rotate(key_rows, cosine_table, sine_table).astype(BF16)
    keys_all, values_all, out_full, lift_out, gate_up, lift_gate_up, down, lift_down = gather(
        [keys_rot, value_rows.astype(BF16)],
        [
            plain_shard(output_projection, output_adapter_in),
            plain_shard(output_adapter_out),
            model_shard(gate_up_weight, gate_up_adapter_in, feedforward_gain),
            plain_shard(gate_up_adapter_out),
            plain_shard(down_weight, down_adapter_in),
            plain_shard(down_adapter_out),
        ],
        1,
    )
    gain_two = gain_whole(gate_up, model_rows)
    length = keys_all.shape[0]
    valid_count = length - pad_lengths[0]
    span = min(512, length)
    bounds = jnp.stack([start_pos, valid_count])

    attended, log_norm = attention_forward(bounds, query_rot, keys_all, values_all, span)
    attended_low = heads_to_columns(attended.astype(BF16))
    out_both = matmul(attended_low, out_full)
    lifted_out = spread(out_both[:, width:].astype(BF16), rank_rows, rank_wide)
    middle = hidden + (out_both[:, :width] + matmul(lifted_out, lift_out))

    normed_two, norm_two_back = jax.vjp(rms_scale, middle, gain_two)
    second_in = spread(normed_two.astype(BF16), model_rows, model_wide)
    pre_gate = matmul(second_in, gate_up)
    lifted_gate_up = spread(pre_gate[:, 2 * FF :].astype(BF16), pair_rows, pair_wide)
    half_gate = lifted_gate_up.shape[1] // 2
    gate_part = pre_gate[:, :FF] + matmul(lifted_gate_up[:, :half_gate], lift_gate_up[:half_gate])
    upper_part = pre_gate[:, FF : 2 * FF] + matmul(
        lifted_gate_up[:, half_gate:], lift_gate_up[half_gate:]
    )
    activated, gelu_back = jax.vjp(partial(jax.nn.gelu, approximate=True), gate_part)
    inner = spread((activated * upper_part).astype(BF16), ff_rows, ff_wide)
    down_both = matmul(inner, down)
    lifted_down = spread(down_both[:, width:].astype(BF16), rank_rows, rank_wide)
    output = middle + (down_both[:, :width] + matmul(lifted_down, lift_down))

    matches = dataset_ids[:, None] == jnp.arange(DATASETS, dtype=jnp.int32)[None, :]
    picked = jnp.sum(jnp.where(matches, mixing[None, :], 0.0), axis=1)
    row_weight = jnp.where(positions < valid_count, picked, 0.0)
    scaled = cotangent.astype(F32) * row_weight[:, None]

    grad_branch = scaled.astype(BF16)
    grad_lifted_down = collect(times_transposed(grad_branch, lift_down), rank_rows, rank_wide)
    grad_down = jnp.concatenate([grad_branch, grad_lifted_down.astype(BF16)], axis=1)
    grad_inner = collect(times_transposed(grad_down, down), ff_rows, ff_wide)
    grad_gate = gelu_back(grad_inner * upper_part)[0].astype(BF16)
    grad_upper = (grad_inner * activated).astype(BF16)
    grad_gate_up = jnp.concatenate(
        [
            grad_gate,
            grad_upper,
            collect(
                times_transposed(grad_gate, lift_gate_up[:half_gate]), pair_rows, pair_wide
            ).astype(BF16),
            collect(
                times_transposed(grad_upper, lift_gate_up[half_gate:]), pair_rows, pair_wide
            ).astype(BF16),
        ],
        axis=1,
    )
    grad_normed_two = collect(times_transposed(grad_gate_up, gate_up), model_rows, model_wide)
    grad_middle_norm, gain_two_grad = norm_two_back(grad_normed_two)
    grad_middle = scaled + grad_middle_norm

    grad_attn = grad_middle.astype(BF16)
    grad_lifted_out = collect(times_transposed(grad_attn, lift_out), rank_rows, rank_wide)
    grad_out = jnp.concatenate([grad_attn, grad_lifted_out.astype(BF16)], axis=1)
    grad_attention = times_transposed(grad_out, out_full).astype(BF16)
    correction = jnp.concatenate(
        [
            jnp.sum(
                grad_attention[:, h * HEAD_DIM : (h + 1) * HEAD_DIM].astype(F32)
                * attended[h * tokens : (h + 1) * tokens],
                axis=1,
            )
            for h in range(HEADS)
        ]
    )
    grad_query_rot, kv_terms = attention_backward(
        bounds,
        query_rot,
        grad_attention,
        keys_all,
        values_all,
        log_norm.reshape(1, -1),
        correction.reshape(1, -1),
        span,
    )
    gate_up_out_term = jnp.concatenate(
        [
            transposed_times(lifted_gate_up[:, :half_gate], grad_gate, BF16),
            transposed_times(lifted_gate_up[:, half_gate:], grad_upper, BF16),
        ],
        axis=0,
    )
    kv_summed, gate_up_sum, down_sum, out_sum, gate_up_out_sum, out_out_sum, down_out_sum = scatter(
        [kv_terms],
        [
            with_gain(transposed_times(second_in, grad_gate_up, BF16), gain_two_grad, model_rows),
            transposed_times(inner, grad_down, BF16),
            transposed_times(attended_low, grad_out, BF16),
            gate_up_out_term,
            transposed_times(lifted_out, grad_attn, BF16),
            transposed_times(lifted_down, grad_branch, BF16),
        ],
        2,
    )
    grad_query_pre = rotate_heads(heads_to_columns(grad_query_rot), cosine_table, -sine_table)
    grad_keys = rotate(kv_summed[:, :HEAD_DIM], cosine_table, -sine_table)
    grad_query_low = grad_query_pre.astype(BF16)
    grad_keys_low = grad_keys.astype(BF16)
    grad_values_low = kv_summed[:, HEAD_DIM:].astype(BF16)
    grad_merged = jnp.concatenate(
        [
            grad_query_low,
            grad_keys_low,
            grad_values_low,
            collect(times_transposed(grad_query_low, lift_query), rank_rows, rank_wide).astype(BF16),
            collect(
                times_transposed(grad_keys_low, lift_keyval[:half_pair]), pair_rows, pair_wide
            ).astype(BF16),
            collect(
                times_transposed(grad_values_low, lift_keyval[half_pair:]), pair_rows, pair_wide
            ).astype(BF16),
        ],
        axis=1,
    )
    grad_normed_one = collect(times_transposed(grad_merged, merged), model_rows, model_wide)
    grad_hidden_norm, gain_one_grad = norm_one_back(grad_normed_one)
    hidden_grad = grad_middle + grad_hidden_norm

    keyval_term = jnp.concatenate(
        [
            transposed_times(lifted_pair[:, :half_pair], grad_keys_low, BF16),
            transposed_times(lifted_pair[:, half_pair:], grad_values_low, BF16),
        ],
        axis=0,
    )
    merged_sum, query_out_sum, keyval_sum = scatter(
        [],
        [
            with_gain(transposed_times(first_in, grad_merged, BF16), gain_one_grad, model_rows),
            transposed_times(lifted_query, grad_query_low, BF16),
            keyval_term,
        ],
        3,
    )
    grads = finish(
        [
            merged_sum,
            query_out_sum,
            keyval_sum,
            out_sum,
            out_out_sum,
            gate_up_sum,
            gate_up_out_sum,
            down_sum,
            down_out_sum,
        ],
        [
            (0, model_rows, 0, merged_width),
            (0, model_rows, merged_width, 3 * RANK),
            (1, rank_rows, 0, query_width),
            (2, pair_rows, 0, HEAD_DIM),
            (3, out_rows, 0, width),
            (3, out_rows, width, RANK),
            (4, rank_rows, 0, width),
            (5, model_rows, 0, 2 * FF),
            (5, model_rows, 2 * FF, 2 * RANK),
            (6, pair_rows, 0, FF),
            (7, ff_rows, 0, width),
            (7, ff_rows, width, RANK),
            (8, rank_rows, 0, width),
        ],
    )
    return (
        output.astype(BF16),
        hidden_grad.astype(BF16),
        merged_sum[model_rows, :model_rows],
        *grads[:7],
        gate_up_sum[model_rows, :model_rows],
        *grads[7:],
    )


def solution(mesh):
    rows, vector = P(AXES, None), P(AXES)
    return jax.shard_map(
        per_device,
        mesh=mesh,
        in_specs=(rows, rows, vector, P(), P("fsdp"), vector)
        + (rows,) * 7
        + (vector,)
        + (rows,) * 6,
        out_specs=(rows, rows, vector) + (rows,) * 7 + (vector,) + (rows,) * 6,
        check_vma=False,
    )
```

time: 549 us -> 430 us (0.78)
  Pallas kernels: 419 us -> 308 us
  local copies, waits for them, and re-layouts: 39.8 us -> 22.9 us
  other arithmetic: 23 us -> 38.4 us
    pallas_call x5, Pallas kernels: 405 us -> 295 us  [the longest x2 153 us: scatter(): pl.pallas_call(partial(scatter_kernel, groups, tuple(plan), tuple(rows_pl...]
    unnamed x17, other arithmetic: 9.69 us -> 17.7 us
    pad x6 -> x0, local copies, waits for them, and re-layouts: 7.98 us -> none  [the longest x4 5.89 us: pad_shard(): return jnp.pad(shard, ((0, padded_rows(rows) - rows), (0, 0)))]
    unnamed x197 -> x111, local copies, waits for them, and re-layouts: 22.2 us -> 14.5 us
    concatenate x1 -> x5, other arithmetic: 0.72 us -> 6.96 us  [the longest x2 3.25 us: model_shard(): return jnp.concatenate([block, spare], axis=0)]
    dot_general x15 -> x11, matrix products: 25.8 us -> 22 us  [transposed_times(): lax.dot_general(left_side, right_side, (((0,), (0,)), ((), ())), preferre...]
    dot_general x21 -> x17, matrix products: 15.1 us -> 16.8 us  [times_transposed(): lax.dot_general(left_side, right_side, (((1,), (1,)), ((), ())), preferre...]
    dot_general x17 -> x13, matrix products: 15.1 us -> 13.9 us  [matmul(): return jnp.dot(left_side, right_side, preferred_element_type=F32)]
where the time goes in v2:
time: 430 us; the launch traced here: 425 us
  Pallas kernels  308 us (72%)
  matrix products  52.6 us (12%)
  other arithmetic  38.4 us (9%)
  local copies, waits for them, and re-layouts  22.9 us (5%)
    pallas_call x2, Pallas kernels, scatter(): pl.pallas_call(partial(scatter_kernel, groups, tuple(plan), tuple(rows_pl...  153 us
    pallas_call x2, Pallas kernels, gather(): pl.pallas_call(partial(gather_kernel, groups, tuple(plan), tuple(rows_pla...  139 us
    dot_general x11, matrix products, transposed_times(): lax.dot_general(left_side, right_side, (((0,), (0,)), ((), ())), preferre...  22 us
    unnamed x17, other arithmetic  17.7 us
    dot_general x17, matrix products, times_transposed(): lax.dot_general(left_side, right_side, (((1,), (1,)), ((), ())), preferre...  16.8 us
    unnamed x111, local copies, waits for them, and re-layouts  14.5 us
    dot_general x13, matrix products, matmul(): return jnp.dot(left_side, right_side, preferred_element_type=F32)  13.9 us

profile of v2, /device:TPU:0, one launch (start us, length us, event | category | flops | bytes accessed | tf_op | source)
XLA Modules:
  0.0 424.8 jit_solution(15969738712731588648)
XLA Ops:
  2.0 1.1 fusion.22
  3.1 0.8 select_reduce_fusion
  3.9 1.4 pad_maximum_fusion.19.refs_2_
  5.4 1.6 fusion.134.refs_0_
  6.9 1.6 pad_maximum_fusion.14.refs_6_
  8.5 1.7 fusion.41.refs_4_
  10.2 1.1 fusion.24
  11.3 35.4 %gather_0.1 = (bf16[2,4,2,2,24,2304]{5,4,3,2,1,0:T(8,128)(2,1)}, bf16[2,4,2,2,8,1024]{5,4,3,2,1,0:T(8,128)(2,1)}, bf16[2,4,2,2,16,256]{5,4,3,2,1,0:T(8,128)(2,1)}) custom-call(bf16[24,2304]{1,0:T(8,128)(2,1)} %fusion.134.refs_0_, bf16[8,1024]{1,0:T(8,128)(2,1)} %refs_1_.1, bf16[16,256]{1,0:T(8,128)(2,1)} %refs_2_.1), custom_call_target="tpu_custom_call" | custom-call | tf_op jit(solution)/shard_map/gather_0/pallas_call | solution.py:331
  46.7 0.9 slice.336
  47.6 1.0 fusion.184
  49.3 1.4 copy-done.4
  50.7 1.1 fusion.185
  51.9 1.1 fusion.11.refs_1_
  59.6 103.3 %gather_1.1 = (bf16[4,2,2,256,256]{4,3,2,1,0:T(8,128)(2,1)}, bf16[4,2,2,256,256]{4,3,2,1,0:T(8,128)(2,1)}, bf16[2,4,2,2,32,896]{5,4,3,2,1,0:T(8,128)(2,1)}, bf16...) custom-call(bf16[256,256]{1,0:T(8,128)(2,1)} %pad_maximum_fusion.12., ...), custom_call_target="tpu_custom_call" | custom-call | tf_op jit(solution)/shard_map/gather_1/pallas_call | solution.py:331
  162.9 0.9 slice.359
  163.9 1.3 convolution_convert_fusion.14
  165.2 6.3 %attention_forward.1 = (f32[1024,256]{1,0:T(8,128)}, f32[1024,1]{1,0:T(8,128)}) custom-call(s32[2]{0:T(128)} %pad_add_fusion.bounds, bf16[256,1024]{1,0:T(8,128)(2,1)} %copy-done.18, bf16[4096,256]{1,0:T(8,128)(2,1)} %bitcast.94, bf16[4096,256]{1,0:T(8,128)(2,1)} %bitcast.96), custom_call_target="tpu_custom_call" | custom-call | tf_op jit(solution)/shard_map/attention_forward/pallas_call | solution.py:638
  171.5 1.8 reduce.4
  173.4 1.3 convert_element_type.217
  174.7 2.4 fusion.135
  178.2 1.0 copy-done.3
  179.2 1.3 fusion.40
  182.2 2.0 fusion.186
  184.7 1.0 copy-done.6
  185.7 2.4 fusion.6
  189.1 2.1 fusion.34
  191.2 1.3 fusion.187
  192.5 1.0 fusion.10
  193.5 1.1 convolution_convert_fusion.10
  195.8 0.8 multiply_reduce_fusion
  196.7 1.1 fusion.180
  197.8 1.1 convolution_convert_fusion.11
  201.0 7.4 %attention_backward.1 = (f32[1024,256]{1,0:T(8,128)}, bf16[4096,512]{1,0:T(8,128)(2,1)}) custom-call(s32[2]{0:T(128)} %pad_add_fusion.bounds, bf16[256,1024]{1,0:T(8,128)(2,1)} %copy-done.18, bf16[256,1024]{1,0:T(8,128)(2,1)} %copy-done.24, bf16[4096,256]{1,0:T(8,128)(2,1)} %bitcast.95, bf16[4096,256]{1,0:T(8,128)(2,1)} %bitcast.97, f32[1,1024]{1,0:T(1,128)} %bitcast.121, ...), custom_call_target="tpu_custom_call" | custom-call | tf_op jit(solution)/shard_map/attention_backward/pallas_call | solution.py:714
  208.5 1.6 constant_dynamic-update-slice_fusion.7
  210.1 1.6 constant_dynamic-update-slice_fusion.6
  211.7 1.6 constant_dynamic-update-slice_fusion.5
  213.3 1.6 constant_dynamic-update-slice_fusion.4
  214.8 1.6 constant_dynamic-update-slice_fusion.3
  218.3 2.2 convolution_convert_fusion.6
  220.5 1.4 convolution_convert_fusion.4
  221.8 1.4 convolution_convert_fusion.3
  223.2 1.6 pad_maximum_fusion.1
  230.0 2.0 convolution_convert_fusion.5
  232.0 3.2 convolution_convert_fusion.2
  235.2 5.1 %convolution_convert_fusion = bf16[768,4608]{1,0:T(8,128)(2,1)} fusion(bf16[256,768]{1,0:T(8,128)(2,1)S(1)} %copy-done.21, bf16[256,256]{1,0:T(8,128)(2,1)S(1)} %copy-done.33, bf16[256,256]{1,0:T(8,128)(2,1)S(1)} %copy-done.35, bf16[256,2048]{1,0:T(8,128)(2,1)S(1)} %get-tuple-element.148, bf16[256,2048]{1,0:T(8,128)(2,1)S(1)} %get-tuple-element.147), kind=kOutput, calls=%fused_computation | convolution fusion | flops 1824915456 | bytes 9830400 | tf_op jit(solution)/shard_map/dot_general | solution.py:64
  240.3 1.9 scatter.6
  242.2 120.5 %scatter_2.1 = (f32[256,512]{1,0:T(8,128)}, f32[24,4608]{1,0:T(8,128)}, f32[64,896]{1,0:T(8,128)}, f32[32,896]{1,0:T(8,128)}, f32[16,2048]{1,0:T(8,128)}, /*index=5*/f32[8,640]{1,0:T(8,128)}, f32[8,640]{1,0:T(8,128)}) custom-call(bf16[4,2,2,256,512]{4,3,2,1,0:T(8,128)(2,1)} %bitcast.98, bf16[2,4,2,2,24,4608]{5,4,3,2,1,0:T(8,128)(2,1)} %bitcast.82, ...), custom_call_target="tpu_custom_call" | custom-call | tf_op jit(solution)/shard_map/scatter_2/pallas_call | solution.py:540
  362.8 1.3 slice_bitcast_fusion
  364.0 2.2 constant_dynamic-update-slice_fusion.10
  366.2 2.1 constant_dynamic-update-slice_fusion.9
  368.4 1.6 constant_dynamic-update-slice_fusion.8
  370.0 2.0 fusion.12
  372.0 0.9 fusion.14
  373.0 0.9 fusion.13
  373.8 2.4 fusion.188
  376.2 1.1 convolution_convert_fusion.15
  377.4 1.1 convolution_convert_fusion.16
  380.8 0.8 fusion.18
  381.9 0.9 fusion.21
  382.9 2.5 convolution_convert_fusion.1
  386.1 1.7 copy-done
  387.9 32.8 %scatter_3.1 = (f32[24,2304]{1,0:T(8,128)}, f32[8,1024]{1,0:T(8,128)}, f32[16,256]{1,0:T(8,128)}) custom-call(bf16[2,4,2,2,24,2304]{5,4,3,2,1,0:T(8,128)(2,1)} %bitcast.85, bf16[2,4,2,2,8,1024]{5,4,3,2,1,0:T(8,128)(2,1)} %bitcast.106, bf16[2,4,2,2,16,256]{5,4,3,2,1,0:T(8,128)(2,1)} %bitcast.118), custom_call_target="tpu_custom_call" | custom-call | tf_op jit(solution)/shard_map/scatter_3/pallas_call | solution.py:540
  420.7 1.2 slice_bitcast_fusion.1
  421.9 2.4 finish.1
  (157 shorter events, 26.3 us)
Async XLA Ops:
  0.7 48.0 %copy-start.7 = (bf16[256,640]{1,0:T(8,128)(2,1)S(1)}, bf16[256,640]{1,0:T(8,128)(2,1)}, u32[]{:S(2)}) copy-start(bf16[256,640]{1,0:T(8,128)(2,1)} %param.24) | copy-start | bytes 983044
  48.6 3.2 copy-start.30
  48.6 4.3 %copy-start.36 = (bf16[1,4,2,2,16,256]{5,4,3,2,1,0:T(8,128)(2,1)}, bf16[1,4,2,2,16,256]{5,4,3,2,1,0:T(8,128)(2,1)S(1)}, u32[]{:S(2)}) copy-start(bf16[1,4,2,2,16,256]{5,4,3,2,1,0:T(8,128)(2,1)S(1)} %get-tuple-element.159) | copy-start | bytes 393220
  48.7 2.1 copy-start.4
  50.7 3.3 copy-start.19
  50.7 2.4 copy-start.23
  51.9 1.6 copy-start.11
  59.6 105.6 %copy-start.18 = (bf16[256,1024]{1,0:T(8,128)(2,1)}, bf16[256,1024]{1,0:T(8,128)(2,1)S(1)}, u32[]{:S(2)}) copy-start(bf16[256,1024]{1,0:T(8,128)(2,1)S(1)} %fusion.136.query_ref) | copy-start | bytes 1572868
  165.2 13.1 %copy-start.28 = (bf16[256,256]{1,0:T(8,128)(2,1)}, bf16[256,256]{1,0:T(8,128)(2,1)S(1)}, u32[]{:S(2)}) copy-start(bf16[256,256]{1,0:T(8,128)(2,1)S(1)} %convolution_convert_fusion.14) | copy-start | bytes 393220
  174.7 2.4 copy-start.40
  174.7 2.4 copy-start.42
  174.7 2.4 copy-start.44
  174.7 2.4 copy-start.46
  174.7 2.4 copy-start.25
  177.2 2.0 copy-start.3
  177.6 3.9 slice-start
  179.2 2.2 copy-start.20
  179.2 2.0 copy-start.22
  179.2 3.0 slice-start.1
  184.2 1.5 copy-start.6
  188.1 3.1 copy-start.12
  188.6 2.6 copy-start.32
  189.1 2.1 copy-start.34
  191.2 1.3 copy-start.26
  195.8 1.0 copy-start.27
  196.7 2.5 copy-start.48
  197.8 2.1 copy-start.9
  198.9 1.2 copy-start.2
  199.2 1.2 copy-start.38
  200.1 0.9 copy-start.24
  208.4 8.1 %copy-start.1 = (f32[1024,256]{1,0:T(8,128)S(1)}, f32[1024,256]{1,0:T(8,128)}, u32[]{:S(2)}) copy-start(f32[1024,256]{1,0:T(8,128)} %get-tuple-element.92) | copy-start | bytes 3145732
  218.3 2.2 copy-start.16
  223.2 6.8 %copy-start.10 = (bf16[256,640]{1,0:T(8,128)(2,1)S(1)}, bf16[256,640]{1,0:T(8,128)(2,1)}, u32[]{:S(2)}) copy-start(bf16[256,640]{1,0:T(8,128)(2,1)} %copy-done.9) | copy-start | bytes 983044
  223.2 6.8 %copy-start.39 = (bf16[256,256]{1,0:T(8,128)(2,1)S(1)}, bf16[256,256]{1,0:T(8,128)(2,1)}, u32[]{:S(2)}) copy-start(bf16[256,256]{1,0:T(8,128)(2,1)} %copy-done.38) | copy-start | bytes 393220
  223.2 6.8 %copy-start.41 = (bf16[256,256]{1,0:T(8,128)(2,1)S(1)}, bf16[256,256]{1,0:T(8,128)(2,1)}, u32[]{:S(2)}) copy-start(bf16[256,256]{1,0:T(8,128)(2,1)} %copy-done.40) | copy-start | bytes 393220
  223.2 6.8 %copy-start.43 = (bf16[256,256]{1,0:T(8,128)(2,1)S(1)}, bf16[256,256]{1,0:T(8,128)(2,1)}, u32[]{:S(2)}) copy-start(bf16[256,256]{1,0:T(8,128)(2,1)} %copy-done.42) | copy-start | bytes 393220
  223.2 6.8 %copy-start.45 = (bf16[256,256]{1,0:T(8,128)(2,1)S(1)}, bf16[256,256]{1,0:T(8,128)(2,1)}, u32[]{:S(2)}) copy-start(bf16[256,256]{1,0:T(8,128)(2,1)} %copy-done.44) | copy-start | bytes 393220
  223.2 6.8 %copy-start.47 = (bf16[256,256]{1,0:T(8,128)(2,1)S(1)}, bf16[256,256]{1,0:T(8,128)(2,1)}, u32[]{:S(2)}) copy-start(bf16[256,256]{1,0:T(8,128)(2,1)} %copy-done.46) | copy-start | bytes 393220
  230.0 2.0 copy-start.13
  230.0 2.0 copy-start.29
  232.0 3.2 copy-start.21
  232.0 3.2 copy-start.33
  232.0 3.2 copy-start.35
  242.2 127.8 %copy-start.17 = (bf16[256,1024]{1,0:T(8,128)(2,1)S(1)}, bf16[256,1024]{1,0:T(8,128)(2,1)}, u32[]{:S(2)}) copy-start(bf16[256,1024]{1,0:T(8,128)(2,1)} %copy-done.16) | copy-start | bytes 1572868
  242.2 131.6 %copy-start.5 = (bf16[2,4,2,2,24,2304]{5,4,3,2,1,0:T(8,128)(2,1)S(1)}, bf16[2,4,2,2,24,2304]{5,4,3,2,1,0:T(8,128)(2,1)}, u32[]{:S(2)}) copy-start(bf16[2,4,2,2,24,2304]{5,4,3,2,1,0:T(8,128)(2,1)} %get-tuple-element.79) | copy-start | bytes 10616836
  362.7 9.3 %copy-start.37 = (bf16[1,4,2,2,16,256]{5,4,3,2,1,0:T(8,128)(2,1)S(1)}, bf16[1,4,2,2,16,256]{5,4,3,2,1,0:T(8,128)(2,1)}, u32[]{:S(2)}) copy-start(bf16[1,4,2,2,16,256]{5,4,3,2,1,0:T(8,128)(2,1)} %copy-done.36) | copy-start | bytes 393220
  362.7 10.2 %copy-start.14 = (f32[256,512]{1,0:T(8,128)S(1)}, f32[256,512]{1,0:T(8,128)}, u32[]{:S(2)}) copy-start(f32[256,512]{1,0:T(8,128)} %get-tuple-element.94) | copy-start | bytes 1572868
  362.8 10.2 %copy-start.31 = (bf16[1,4,2,2,16,256]{5,4,3,2,1,0:T(8,128)(2,1)S(1)}, bf16[1,4,2,2,16,256]{5,4,3,2,1,0:T(8,128)(2,1)}, u32[]{:S(2)}) copy-start(bf16[1,4,2,2,16,256]{5,4,3,2,1,0:T(8,128)(2,1)} %copy-done.30) | copy-start | bytes 393220
  379.8 1.0 copy-start.8
  380.8 1.1 copy-start.15
  386.1 1.8 copy-start
